TPU v7x, 32 devices: a whole 2x2x4 slice. The times are simulated.
32 devices in a mesh: row: 16 (over z, y, x), col: 2 (over core).
Axes of the slice: x: 2, y: 2, z: 4, core: 2. Of those that a mesh axis runs over, the one named last changes fastest.
Arguments:
- vectors_in: bfloat16 [32768, 2048], P('row', 'col'), may hold values from -6 to 6
- panel: bfloat16 [32768, 256], P('row', 'col'), may hold values from -0.03125 to 0.03125
- factor: float32 [256, 256], replicated, may hold values from -3 to 8, as said below
- atom_basis: int32 [16, 128], P('row'), may hold values from 1 to 24, 2048 in all within a row
- proj_count: int32 [2048], P('row'), may hold values from 1 to 16
- coupling: bfloat16 [2048, 9, 384], P('row'), may hold values from -0.4375 to 0.4375
- block_present: int32 [2048, 9], P('row'), may hold values 0 or 1
- occ_mask: int32 [2048], P('col'), may hold values 0 or 1
- occ_weight: float32 [2048], P('col'), may hold values from 0.5 to 2
Outputs:
- vectors: bfloat16 [32768, 2048], P('row', 'col')
- density: float32 [2048, 256], P(('row', 'col'))
Inputs may be any that keep to these rules, and one draw needn't show every extreme that they name: `factor`: zero below the diagonal; the diagonal lies in 4 to 8. `atom_basis`: each row sums to 2048, and 24 is reached in each row.
All inputs are finite; a program needn't handle non-finite values. No bound on the sum of `block_present` or of `occ_mask` on one device may be relied on, other than what follows from the above.
Results may differ from a plain program's by a relative error of at most 0.0075.
Values may be sent and summed in bfloat16 or wider, within the bound.
A program may use at most 192 MiB of HBM per device.

v0:
```python
import functools

import jax
import jax.numpy as jnp
from jax import lax
from jax.experimental import pallas as pl
from jax.experimental.pallas import tpu as pltpu
from jax.sharding import PartitionSpec as P

NPMAX = 16
BMAX = 24
K = 9
RIM = (K - 1) // 2
HALO = RIM * BMAX
GROUP = 16
WIN = -(-(GROUP + K - 1) * BMAX // 128) * 128
FOLD = -(-K * BMAX // 128) * 128
F32 = jnp.float32
BF16 = jnp.bfloat16
MESH = pl.DeviceIdType.MESH


def iota(rows, columns, axis):
    return lax.broadcasted_iota(jnp.int32, (rows, columns), axis)


def group_of(rows, columns, axis, size, most):
    small = (8, columns) if axis == 1 else (rows, 128)
    index = iota(*small, axis)
    group = jnp.zeros(small, jnp.int32)
    for edge in range(1, most):
        group = group + jnp.where(index >= edge * size, 1, 0)
    return jnp.tile(group, (rows // small[0], columns // small[1]))


def mix_kernel(n, plane, vec_hbm, panel_hbm, coupling_hbm, factor_ref, basis_ref, proj_ref, present_ref,
               mix_ref, pan_ref, base_ref, lean_ref,
               vec, part, got, middle, got_line, counts, limit, spread, fold, cm_ref, halo_ref, band, first_ref, starts,
               ext, pext, padded, ppadded,
               load_sem, own_sem, cm_sem, start_sem, pan_sems, halo_sems, count_sems, plane_sems, line_sems, mix_sems, pass_sems):
    row, col = lax.axis_index("row"), lax.axis_index("col")
    other = 1 - col
    up, down = lax.rem(row + 1, n), lax.rem(row + n - 1, n)
    rows, half = panel_hbm.shape
    slab = mix_ref.shape[0] // n
    body = pl.ds(HALO, rows)
    q, p = n // plane, plane
    line, spot = lax.div(row, p), lax.rem(row, p)

    def plane_peer(step):
        return line * p + lax.rem(spot + step, p)

    def line_peer(step):
        return lax.rem(line + step, q) * p + spot


    own = pltpu.make_async_copy(panel_hbm, pan_ref.at[col, body], own_sem)
    own.start()
    early = pl.ds(0, rows // 2)
    late = pl.ds(rows // 2, rows // 2)
    loads = [pltpu.make_async_copy(vec_hbm.at[part_rows], vec.at[part_rows], load_sem.at[i])
             for i, part_rows in enumerate((early, late))]
    for load in loads:
        load.start()
    blocks = pltpu.make_async_copy(coupling_hbm, cm_ref, cm_sem)
    blocks.start()

    barrier = pltpu.get_barrier_semaphore()
    greeted = [(plane_peer(step), col) for step in range(1, p)] + [(line_peer(step), col) for step in range(1, q)]
    greeted += [(up, col), (down, col)] + [(peer, other) for peer in (row, up, down)]
    for target in greeted:
        pl.semaphore_signal(barrier, inc=1, device_id=target, device_id_type=MESH)
    atoms, wide = cm_ref.shape[1:]
    spread[...] = jnp.where(group_of(GROUP * NPMAX, wide, 1, BMAX, NPMAX) == (iota(GROUP * NPMAX, wide, 0) & 15),
                            1.0, 0.0)
    fold_slot = iota(wide, FOLD, 1) - BMAX * group_of(wide, FOLD, 1, BMAX, K)
    fold_from = iota(wide, FOLD, 0) - BMAX * group_of(wide, FOLD, 0, BMAX, NPMAX)
    fold[...] = jnp.where((fold_slot == fold_from) & (iota(wide, FOLD, 1) < K * BMAX), 1.0, 0.0).astype(BF16)
    own.wait()
    loads[0].wait()
    ahead = lax.dot_general(pan_ref[col, HALO:HALO + rows // 2, :], vec[early, :], (((0,), (0,)), ((), ())),
                            preferred_element_type=F32)
    pl.semaphore_wait(barrier, len(greeted))

    def remote(src, dst, sems, slot, target):
        return pltpu.make_async_remote_copy(
            src_ref=src, dst_ref=dst, send_sem=sems.at[(0,) + slot], recv_sem=sems.at[(1,) + slot],
            device_id=target, device_id_type=MESH)

    swap = remote(panel_hbm, pan_ref.at[col, pl.ds(HALO, rows)], pan_sems, (0,), (row, other))
    swap.start()
    count_copies = [
        remote(basis_ref, counts.at[side], count_sems, (side,), (target, col))
        for side, target in ((0, up), (1, down))
    ]
    for copy in count_copies:
        copy.start()
    halos = []
    for side, target in ((0, up), (1, down)):
        src_at = rows - HALO if side == 0 else 0
        dst_at = 0 if side == 0 else HALO + rows
        for where in (0, 1):
            to = col if where == 0 else other
            halos.append(remote(panel_hbm.at[pl.ds(src_at, HALO)], pan_ref.at[col, pl.ds(dst_at, HALO)],
                                pan_sems, (1 + 2 * side + where,), (target, to)))
        halos.append(remote(vec_hbm.at[pl.ds(src_at, HALO)], halo_ref.at[side], halo_sems, (side,), (target, col)))
    loads[1].wait()

    def product(which, piece):
        piece = piece.T.astype(BF16)
        for z in range(q):
            for at in range(p):
                part[which, at, z * slab:(z + 1) * slab] = piece[(z * p + at) * slab:(z * p + at + 1) * slab]

    def plane_copy(which, step):
        return remote(part.at[which, lax.rem(spot + step, p)], got.at[which, step], plane_sems, (which, step),
                      (plane_peer(step), col))

    def line_copy(which, step):
        at = pl.multiple_of(lax.rem(line + step, q) * slab, slab)
        return remote(middle.at[which, pl.ds(at, slab)], got_line.at[which, step], line_sems, (which, step),
                      (line_peer(step), col))

    contract = (((0,), (0,)), ((), ()))
    product(col, ahead + lax.dot_general(pan_ref[col, HALO + rows // 2:HALO + rows, :], vec[late, :], contract,
                                         preferred_element_type=F32))
    for step in range(1, p):
        plane_copy(col, step).start()
    swap.wait_recv()
    product(other, lax.dot_general(pan_ref[other, HALO:HALO + rows, :], vec[...], contract,
                                   preferred_element_type=F32))
    for step in range(1, p):
        plane_copy(other, step).start()
    for copy in halos:
        copy.start()

    for copy in count_copies:
        copy.wait_recv()
    blocks.wait()
    here = basis_ref[...].astype(F32)
    prev, post = counts[0].astype(F32), counts[1].astype(F32)
    lower = jnp.where(iota(atoms, atoms, 0) < iota(atoms, atoms, 1), 1.0, 0.0).astype(BF16)
    table = jnp.concatenate([prev, here, post, jnp.zeros((5, atoms), F32)], axis=0).astype(BF16)
    first = jnp.dot(table, lower, preferred_element_type=F32).astype(jnp.int32)
    first_ref[...] = jnp.clip(first + (HALO - rows) + rows * iota(8, atoms, 0), 0, rows + 2 * HALO)
    begin_copy = pltpu.make_async_copy(first_ref, starts, start_sem)
    begin_copy.start()
    lines = []
    at = iota(1, atoms, 1)
    for k in range(K):
        d = k - RIM
        near = here
        if d != 0:
            turn = (-d) % atoms
            inside = (at + d >= 0) & (at + d < atoms)
            near = jnp.where(inside, pltpu.roll(here, turn, 1), pltpu.roll(prev if d < 0 else post, turn, 1))
        lines.append(jnp.where(present_ref[k:k + 1, :] > 0, near, 0.0))
    lines.append(proj_ref[...].astype(F32))
    lines.append(jnp.zeros((atoms - K - 1, atoms), F32))
    limit[...] = jnp.concatenate(lines, axis=0).T

    lane = iota(GROUP, FOLD, 1)
    in_k = group_of(GROUP, FOLD, 1, BMAX, K)
    slot = (lane - BMAX * in_k).astype(F32)

    def band_step(t, carry):
        chunk = pl.ds(pl.multiple_of(t * GROUP, GROUP), GROUP)
        bounds = limit[chunk, :]
        reach = jnp.zeros((GROUP, FOLD), F32)
        for k in range(K):
            reach = jnp.where(in_k == k, bounds[:, k:k + 1], reach)
        kept = jnp.where(slot < reach, 1.0, 0.0)
        kept = jnp.broadcast_to(kept[:, None, :], (GROUP, NPMAX, FOLD)).reshape(GROUP * NPMAX, FOLD)
        most = jnp.broadcast_to(bounds[:, K:K + 1], (GROUP, FOLD))
        most = jnp.broadcast_to(most[:, None, :], (GROUP, NPMAX, FOLD)).reshape(GROUP * NPMAX, FOLD)
        valid = (kept > 0.5) & ((iota(GROUP * NPMAX, FOLD, 0) & 15).astype(F32) < most)
        which_k = group_of(GROUP * NPMAX, FOLD, 1, BMAX, K)
        acc = jnp.zeros((GROUP * NPMAX, FOLD), F32)
        for k in range(K):
            block = cm_ref[k, chunk, :].astype(F32)
            block = jnp.broadcast_to(block[:, None, :], (GROUP, NPMAX, wide)).reshape(GROUP * NPMAX, wide)
            folded = jnp.dot((block * spread[...]).astype(BF16), fold[...], preferred_element_type=F32)
            acc = jnp.where(which_k == k, folded, acc)
        acc = jnp.where(valid, acc, 0.0)
        acc = jnp.concatenate([acc, jnp.zeros((acc.shape[0], WIN - FOLD), F32)], axis=1)
        pieces = []
        for a in range(GROUP):
            piece = acc[a * NPMAX:(a + 1) * NPMAX]
            pieces.append(piece if a == 0 else pltpu.roll(piece, a * BMAX, 1))
        band[t] = jnp.concatenate(pieces, axis=0).astype(BF16)
        return carry

    lax.fori_loop(0, atoms // GROUP, band_step, 0)

    for which in (0, 1):
        total = part[which, spot].astype(F32)
        for step in range(1, p):
            plane_copy(which, step).wait_recv()
            total = total + got[which, step].astype(F32)
        middle[which] = total.astype(BF16)
        for step in range(1, q):
            line_copy(which, step).start()

    begin_copy.wait()
    for copy in halos:
        copy.wait()
    length = ext.shape[1]
    lanes = [slice(c * 128, (c + 1) * 128) for c in range(ext.shape[0])]
    chunk_rows = rows // 8

    def widen(t, carry):
        at = pl.multiple_of(t * chunk_rows, 16)
        block = vec[pl.ds(at, chunk_rows), :].astype(F32)
        for c, span in enumerate(lanes):
            ext[c, pl.ds(HALO + at, chunk_rows), :] = block[:, span]
        return carry

    lax.fori_loop(0, 8, widen, 0)
    for side, at in ((0, 0), (1, HALO + rows)):
        block = halo_ref[side].astype(F32)
        for c, span in enumerate(lanes):
            ext[c, at:at + HALO, :] = block[:, span]
    spare = length - 2 * HALO - rows
    ext[:, length - spare:, :] = jnp.zeros((ext.shape[0], spare, 128), F32)
    for which in (0, 1):
        pext[which, 0:length - spare, :] = pan_ref[which].astype(F32)
    pext[:, length - spare:, :] = jnp.zeros((2, spare, half), F32)
    used = (atoms + 2 * RIM) * BMAX
    padded[used:, :] = jnp.zeros((padded.shape[0] - used, padded.shape[1]), BF16)
    ppadded[used:, :] = jnp.zeros((ppadded.shape[0] - used, ppadded.shape[1]), BF16)

    mine = pl.ds(pl.multiple_of(row * slab, slab), slab)
    sums = []
    for which in (0, 1):
        total = middle[which, pl.ds(pl.multiple_of(line * slab, slab), slab), :].astype(F32)
        for step in range(1, q):
            line_copy(which, step).wait_recv()
            total = total + got_line[which, step].astype(F32)
        sums.append(total)
    inner = jnp.concatenate(sums, axis=1)
    mixed = jnp.dot(inner, factor_ref[...], precision=lax.Precision.HIGHEST, preferred_element_type=F32)
    mix_ref[mine, :] = mixed.astype(BF16)

    def mix_copy(step):
        return remote(mix_ref.at[mine], mix_ref.at[mine], mix_sems, (step,), (line_peer(step), col))

    def pass_copy(z, step):
        at = pl.multiple_of((lax.rem(line + q - z, q) * p + spot) * slab, slab)
        return remote(mix_ref.at[pl.ds(at, slab)], mix_ref.at[pl.ds(at, slab)], pass_sems, (z, step),
                      (plane_peer(step), col))

    for step in range(1, q):
        mix_copy(step).start()
    for step in range(1, p):
        pass_copy(0, step).start()

    def gather(t, carry):
        at = pl.multiple_of(2 * t * BMAX, 16)
        begins = []
        for e in (0, 1):
            flat = 2 * t + e + atoms - RIM
            begins.append(starts[lax.div(flat, atoms), lax.rem(flat, atoms)])
        for c, span in enumerate(lanes):
            both = [ext[c, pl.ds(begin, BMAX), :] for begin in begins]
            padded[pl.ds(at, 2 * BMAX), span] = jnp.concatenate(both, axis=0).astype(BF16)
        for c in (0, 1):
            both = [pext[c, pl.ds(begin, BMAX), :] for begin in begins]
            ppadded[pl.ds(at, 2 * BMAX), c * half:(c + 1) * half] = jnp.concatenate(both, axis=0).astype(BF16)
        return carry

    lax.fori_loop(0, (atoms + 2 * RIM) // 2, gather, 0)

    for z in range(1, q):
        mix_copy(z).wait_recv()
        for step in range(1, p):
            pass_copy(z, step).start()

    def project(g, carry):
        at = pl.ds(pl.multiple_of(g * GROUP * BMAX, 16), WIN)
        base_ref[g] = jnp.dot(band[g], padded[at, :], preferred_element_type=F32)
        lean_ref[g] = jnp.dot(band[g], ppadded[at, :], preferred_element_type=F32).astype(BF16)
        return carry

    lax.fori_loop(0, atoms // GROUP, project, 0)
    swap.wait_send()
    for copy in count_copies:
        copy.wait_send()
    for which in (0, 1):
        for step in range(1, p):
            plane_copy(which, step).wait_send()
        for step in range(1, q):
            line_copy(which, step).wait_send()
    for step in range(1, q):
        mix_copy(step).wait_send()
    for z in range(q):
        for step in range(1, p):
            pass_copy(z, step).wait()


def density_kernel(vin_ref, pan_ref, mix_ref, base_ref, lean_ref, mask_ref, occ_ref,
                   vec_ref, den_ref, mixing, weight, *, column_total):
    step = pl.program_id(0)
    tile = vin_ref.shape[0]

    @pl.when(step == 0)
    def _():
        mixing[...] = mix_ref[...].T
        weight[...] = mask_ref[...].astype(F32) * occ_ref[...] / column_total

    at = pl.ds(pl.multiple_of(HALO + step * tile, 16), tile)
    panel = jnp.concatenate([pan_ref[0, at, :], pan_ref[1, at, :]], axis=1)
    update = jnp.dot(panel, mixing[...], preferred_element_type=F32)
    vec_ref[...] = (vin_ref[...].astype(F32) - update).astype(BF16)
    update = jnp.dot(lean_ref[step], mixing[...], preferred_element_type=F32)
    rounded = (base_ref[step] - update).astype(BF16)
    weighted = (rounded.astype(F32) * weight[...]).astype(BF16)
    full = lax.dot_general(weighted, rounded, (((1,), (1,)), ((), ())), preferred_element_type=F32)
    shape = full.shape
    full = jnp.where(iota(*shape, 0) >> 4 == iota(*shape, 1) >> 4, full, 0.0)
    expand = jnp.where((iota(shape[1], NPMAX * NPMAX, 0) & 15) == (iota(shape[1], NPMAX * NPMAX, 1) & 15),
                       1.0, 0.0).astype(BF16)
    spreads = 0.0
    for _ in range(3):
        top = full.astype(BF16)
        spreads = spreads + jnp.dot(top, expand, preferred_element_type=F32)
        full = full - top.astype(F32)
    shape = spreads.shape
    spreads = jnp.where((iota(*shape, 0) & 15) == iota(*shape, 1) >> 4, spreads, 0.0)
    den_ref[...] = spreads.reshape(GROUP, NPMAX, shape[1]).sum(axis=1)


def local(vectors_in, panel, factor, atom_basis, proj_count, coupling, block_present, occ_mask, occ_weight):
    n = lax.axis_size("row")
    rows, cols = vectors_in.shape
    half = panel.shape[1]
    npan = factor.shape[0]
    atoms = atom_basis.shape[1]
    groups = atoms // GROUP
    vmem = pl.BlockSpec(memory_space=pltpu.VMEM)
    hbm = pl.BlockSpec(memory_space=pl.ANY)
    slab = cols // n
    plane = max(d for d in range(1, n + 1) if n % d == 0 and d * d <= n)
    ext_rows = rows + 2 * HALO
    pad_rows = (groups - 1) * GROUP * BMAX + WIN
    dma = pltpu.SemaphoreType.DMA
    operands = (vectors_in, panel, jnp.swapaxes(coupling, 0, 1), factor, atom_basis, proj_count[None, :], block_present.T)
    operands = [pltpu.with_memory_space_constraint(x, pltpu.HBM) for x in operands]
    mix, pan, base, lean = pl.pallas_call(
        functools.partial(mix_kernel, n, plane),
        out_shape=(
            jax.ShapeDtypeStruct((cols, npan), BF16),
            jax.ShapeDtypeStruct((2, ext_rows, half), BF16),
            jax.ShapeDtypeStruct((groups, GROUP * NPMAX, cols), F32),
            jax.ShapeDtypeStruct((groups, GROUP * NPMAX, npan), BF16),
        ),
        in_specs=[hbm] * 3 + [vmem] * 4,
        out_specs=(vmem,) * 4,
        scratch_shapes=[
            pltpu.VMEM((rows, cols), BF16),
            pltpu.VMEM((2, plane, cols // plane, half), BF16),
            pltpu.VMEM((2, plane, cols // plane, half), BF16),
            pltpu.VMEM((2, cols // plane, half), BF16),
            pltpu.VMEM((2, n // plane, slab, half), BF16),
            pltpu.VMEM((2, 1, atoms), jnp.int32),
            pltpu.VMEM((atoms, atoms), F32),
            pltpu.VMEM((GROUP * NPMAX, NPMAX * BMAX), F32),
            pltpu.VMEM((NPMAX * BMAX, FOLD), BF16),
            pltpu.VMEM((K, atoms, NPMAX * BMAX), BF16),
            pltpu.VMEM((2, HALO, cols), BF16),
            pltpu.VMEM((groups, GROUP * NPMAX, WIN), BF16),
            pltpu.VMEM((8, atoms), jnp.int32),
            pltpu.SMEM((8, atoms), jnp.int32),
            pltpu.VMEM((cols // 128, ext_rows + BMAX, 128), F32),
            pltpu.VMEM((2, ext_rows + BMAX, half), F32),
            pltpu.VMEM((pad_rows, cols), BF16),
            pltpu.VMEM((pad_rows, npan), BF16),
            dma((2,)), dma, dma, dma, dma((2, 5)), dma((2, 2)), dma((2, 2)),
            dma((2, 2, plane)), dma((2, 2, n // plane)), dma((2, n // plane)), dma((2, n // plane, plane)),
        ],
        compiler_params=pltpu.CompilerParams(collective_id=0, has_side_effects=True, vmem_limit_bytes=40 << 20),
        cost_estimate=pl.CostEstimate(flops=8 * 10**9, bytes_accessed=10 << 20, transcendentals=0),
    )(*operands)

    tile = rows // groups
    vectors, partial = pl.pallas_call(
        functools.partial(density_kernel, column_total=cols * lax.axis_size("col")),
        out_shape=(
            jax.ShapeDtypeStruct((rows, cols), BF16),
            jax.ShapeDtypeStruct((atoms, NPMAX * NPMAX), F32),
        ),
        grid=(groups,),
        in_specs=[pl.BlockSpec((tile, cols), lambda s: (s, 0))] + [vmem] * 6,
        out_specs=[
            pl.BlockSpec((tile, cols), lambda s: (s, 0)),
            pl.BlockSpec((GROUP, NPMAX * NPMAX), lambda s: (s, 0)),
        ],
        scratch_shapes=[pltpu.VMEM((npan, cols), BF16), pltpu.VMEM((1, cols), F32)],
        compiler_params=pltpu.CompilerParams(vmem_limit_bytes=16 << 20),
        cost_estimate=pl.CostEstimate(flops=6 * 10**9, bytes_accessed=10 << 20, transcendentals=0),
    )(operands[0], pan, mix, base, lean, occ_mask[None, :], occ_weight[None, :])

    ncol = lax.axis_size("col")
    share = atoms // ncol
    col = lax.axis_index("col")
    density = lax.dynamic_slice_in_dim(partial, col * share, share, 0)
    for step in range(1, ncol):
        sent = lax.dynamic_slice_in_dim(partial, lax.rem(col + step, ncol) * share, share, 0)
        density = density + lax.ppermute(sent, "col", [(i, (i + step) % ncol) for i in range(ncol)])
    return (vectors, density)


def solution(mesh):
    placed = (
        P("row", "col"),
        P("row", "col"),
        P(),
        P("row", None),
        P("row"),
        P("row", None, None),
        P("row", None),
        P("col"),
        P("col"),
    )
    return jax.shard_map(
        local,
        mesh=mesh,
        in_specs=placed,
        out_specs=(P("row", "col"), P(("row", "col"), None)),
        check_vma=False,
    )
```

profile of v0, /device:TPU:0, one launch (start us, length us, event | category | flops | bytes accessed | tf_op | source)
XLA Modules:
  0.0 49.5 jit_solution(3367537360516977664)
XLA Ops:
  0.6 0.0 copy-start
  0.7 0.0 copy-start.1
  0.7 37.2 %shard_map.104 = (bf16[1024,256]{1,0:T(8,128)(2,1)S(1)}, bf16[2,2240,128]{2,1,0:T(8,128)(2,1)S(1)}, f32[8,256,1024]{2,1,0:T(8,128)S(1)}, bf16[8,256,256]{2,1,0:T(8,128)(2,1)S(1)}) custom-call(bf16[2048,1024]{1,0:T(8,128)(2,1)} %vin_ref.1, bf16[2048,128]{1,0:T(8,128)(2,1)} %panel_hbm.1, bf16[9,128,384]{2,1,0:T(8,128)(2,1)} %bitcast.7, f32[256,256]{1,0:T(8,128)} %factor_ref.1, ...), custom_call_target="tpu_custom_call" | custom-call | flops 8000000000 | bytes 10485760 | tf_op jit(solution)/shard_map/pallas_call | solution.py:348
  37.9 0.0 copy-done
  37.9 0.0 copy-done.1
  37.9 9.7 %shard_map.105 = (bf16[2048,1024]{1,0:T(8,128)(2,1)}, f32[128,256]{1,0:T(8,128)S(1)}) custom-call(bf16[2048,1024]{1,0:T(8,128)(2,1)} %vin_ref.1, bf16[2,2240,128]{2,1,0:T(8,128)(2,1)S(1)} %get-tuple-element.8.pan_ref, bf16[1024,256]{1,0:T(8,128)(2,1)S(1)} %get-tuple-element.9.mix_ref, f32[8,256,1024]{2,1,0:T(8,128)S(1)} %get-tuple-element.10.base_ref, ...), custom_call_target="tpu_custom_call" | custom-call | flops 6000000000 | bytes 10485760 | tf_op jit(solution)/shard_map/pallas_call | solution.py:385
  47.6 0.0 collective-permute-start
  47.6 1.2 %collective-permute-done = f32[64,256]{1,0:T(8,128)S(1)} collective-permute-done((f32[64,256]{1,0:T(8,128)S(1)}, f32[64,256]{1,0:T(8,128)S(1)}, u32[]{:S(2)}, u32[]{:S(2)}) %collective-permute-start) | collective-permute-done | bytes 65568 | tf_op jit(solution)/shard_map/ppermute | solution.py:408
  48.9 0.6 %dynamic-slice_add_fusion = f32[64,256]{1,0:T(8,128)} fusion(f32[64,256]{1,0:T(8,128)S(1)} %collective-permute-done, f32[128,256]{1,0:T(8,128)S(1)} %get-tuple-element.13, s32[]{:T(128)S(6)} %select_n.6), kind=kLoop, calls=%fused_computation | loop fusion | flops 16384 | bytes 196612 | tf_op jit(solution)/shard_map/add | solution.py:408
  (1 shorter events, 0.0 us)
Async XLA Ops:
  0.6 37.2 %copy-start = (s32[1024]{0:T(1024)S(1)}, s32[1024]{0:T(1024)}, u32[]{:S(2)}) copy-start(s32[1024]{0:T(1024)} %param.16) | copy-start | bytes 12292
  0.7 37.2 %copy-start.1 = (f32[1024]{0:T(1024)S(1)}, f32[1024]{0:T(1024)}, u32[]{:S(2)}) copy-start(f32[1024]{0:T(1024)} %param.17) | copy-start | bytes 12292
  47.6 1.3 %collective-permute-start = (f32[64,256]{1,0:T(8,128)S(1)}, f32[64,256]{1,0:T(8,128)S(1)}, u32[]{:S(2)}, u32[]{:S(2)}) collective-permute-start(f32[64,256]{1,0:T(8,128)S(1)} %constant_dynamic-slice_fusion), channel_id=1, source_target_pairs={{0,1},{1,0},{2,3},{3,2},{4,5},{5,4},{6,7},{7,6},{8,9},{9,8},{10,11... | collective-permute-start | bytes 196616 | tf_op jit(solution)/shard_map/ppermute | solution.py:408
where the time goes:
time: 49.8 us; the launch traced here: 49.5 us
  Pallas kernels  46.9 us (94%)
  waiting for transfers between devices  1.24 us (2%)
  between operations  0.7 us (1%)
  other arithmetic  0.64 us (1%)
    pallas_call x1, Pallas kernels, local(): pl.pallas_call(functools.partial(mix_kernel, n, plane), out_shape=(jax.Sh...  37.2 us
    pallas_call x1, Pallas kernels, local(): pl.pallas_call(functools.partial(density_kernel, column_total=cols * lax....  9.67 us
    ppermute x1, waiting for transfers between devices, local(): lax.ppermute(sent, 'col', [(i, (i + step) % ncol) for i in range(ncol)])  1.24 us
  transfers between devices with their start and end apart: 1, of which 1 were waited for; matrix products, arithmetic and copies ran while one was open for 0% of the time, Pallas kernels for 0%

commit v1 on v0

v1 whole, which is shorter than its diff:
```python
import functools

import jax
import jax.numpy as jnp
from jax import lax
from jax.experimental import pallas as pl
from jax.experimental.pallas import tpu as pltpu
from jax.sharding import PartitionSpec as P

NPMAX = 16
BMAX = 24
K = 9
RIM = (K - 1) // 2
HALO = RIM * BMAX
GROUP = 16
WIN = -(-(GROUP + K - 1) * BMAX // 128) * 128
REACH = GROUP + K - 1
F32 = jnp.float32
BF16 = jnp.bfloat16
MESH = pl.DeviceIdType.MESH


def iota(rows, columns, axis):
    return lax.broadcasted_iota(jnp.int32, (rows, columns), axis)


def group_of(rows, columns, axis, size, most):
    small = (8, columns) if axis == 1 else (rows, 128)
    index = iota(*small, axis)
    group = jnp.zeros(small, jnp.int32)
    for edge in range(1, most):
        group = group + jnp.where(index >= edge * size, 1, 0)
    return jnp.tile(group, (rows // small[0], columns // small[1]))


def mix_kernel(n, plane, vec_hbm, panel_hbm, coupling_hbm, factor_ref, basis_ref, proj_ref, present_ref, mask_ref, occ_ref,
               vec, pan_ref, mix_ref, own_ref, got_ref,
               pan_t, part, got_first, middle, got_second, factor_hi, factor_lo, counts, limit, cm_ref, halo_ref, skew, band,
               first_ref, starts, ext, pext, padded, ppadded, base, lean, full, dens, weight,
               load_sem, own_sem, cm_sem, start_sem, pan_sems, halo_sems, count_sems, ring_sems, den_sems):
    row, col = lax.axis_index("row"), lax.axis_index("col")
    other = 1 - col
    up, down = lax.rem(row + 1, n), lax.rem(row + n - 1, n)
    rows, half = panel_hbm.shape
    chunks, wide_c, npan = part.shape
    unit = wide_c // n
    atoms, wide = cm_ref.shape[1:]
    groups = atoms // GROUP
    body = pl.ds(HALO, rows)
    q, p = n // plane, plane
    line, spot = lax.div(row, p), lax.rem(row, p)
    contract = (((0,), (0,)), ((), ()))
    across = (((1,), (1,)), ((), ()))

    def plane_peer(step):
        return line * p + lax.rem(spot + step, p)

    def line_peer(step):
        return lax.rem(line + step, q) * p + spot

    by_plane, by_line = (p, spot, plane_peer), (q, line, line_peer)
    ways = [(by_line, by_plane) if chunks > 2 and c == 0 else (by_plane, by_line) for c in range(chunks)]

    own = pltpu.make_async_copy(panel_hbm, pan_ref.at[col, body], own_sem)
    own.start()
    pieces = rows // load_sem.shape[0]
    loads = [pltpu.make_async_copy(vec_hbm.at[pl.ds(i * pieces, pieces)], vec.at[pl.ds(i * pieces, pieces)], load_sem.at[i])
             for i in range(load_sem.shape[0])]
    for load in loads:
        load.start()
    blocks = pltpu.make_async_copy(coupling_hbm, cm_ref, cm_sem)
    blocks.start()

    barrier = pltpu.get_barrier_semaphore()
    greeted = [(plane_peer(step), col) for step in range(1, p)] + [(line_peer(step), col) for step in range(1, q)]
    greeted += [(up, col), (down, col)] + [(peer, other) for peer in (row, up, down)]
    for target in greeted:
        pl.semaphore_signal(barrier, inc=1, device_id=target, device_id_type=MESH)
    high = factor_ref[...].astype(BF16)
    factor_hi[...] = high
    factor_lo[...] = (factor_ref[...] - high.astype(F32)).astype(BF16)
    weight[...] = mask_ref[...].astype(F32) * occ_ref[...] / (vec_hbm.shape[1] * lax.axis_size("col"))
    length = ext.shape[1]
    edge = rows + HALO
    ext[:, edge:, :] = jnp.zeros((ext.shape[0], length - edge, 128), F32)
    pext[:, edge:, :] = jnp.zeros((2, length - edge, half), F32)
    used = (atoms + 2 * RIM) * BMAX
    padded[used:, :] = jnp.zeros((padded.shape[0] - used, padded.shape[1]), BF16)
    ppadded[used:, :] = jnp.zeros((ppadded.shape[0] - used, ppadded.shape[1]), BF16)
    low = (GROUP - 1) * GROUP
    skew[:, 0:low, :] = jnp.zeros((skew.shape[0], low, 128), F32)
    skew[:, low + K * GROUP:, :] = jnp.zeros((skew.shape[0], low, 128), F32)
    pl.semaphore_wait(barrier, len(greeted))

    def remote(src, dst, sems, slot, target):
        return pltpu.make_async_remote_copy(
            src_ref=src, dst_ref=dst, send_sem=sems.at[(0,) + slot], recv_sem=sems.at[(1,) + slot],
            device_id=target, device_id_type=MESH)

    swap = remote(panel_hbm, pan_ref.at[col, body], pan_sems, (0,), (row, other))
    swap.start()
    count_copies = [
        remote(basis_ref, counts.at[side], count_sems, (side,), (target, col))
        for side, target in ((0, up), (1, down))
    ]
    for copy in count_copies:
        copy.start()
    pan_halos, vec_halos = [], []
    for side, target in ((0, up), (1, down)):
        src_at = rows - HALO if side == 0 else 0
        dst_at = 0 if side == 0 else HALO + rows
        for where in (0, 1):
            to = col if where == 0 else other
            pan_halos.append(remote(panel_hbm.at[pl.ds(src_at, HALO)], pan_ref.at[col, pl.ds(dst_at, HALO)],
                                    pan_sems, (1 + 2 * side + where,), (target, to)))
        vec_halos.append(remote(vec_hbm.at[pl.ds(src_at, HALO)], halo_ref.at[side], halo_sems, (side,), (target, col)))
    for copy in pan_halos:
        copy.start()

    own.wait()
    pan_t[pl.ds(pl.multiple_of(col * half, half), half), :] = pan_ref[col, body, :].T
    for load in loads:
        load.wait()

    lanes = [slice(c * 128, (c + 1) * 128) for c in range(ext.shape[0])]
    chunk_rows = rows // 8

    def widen(t, carry):
        at = pl.multiple_of(t * chunk_rows, 16)
        block = vec[pl.ds(at, chunk_rows), :].astype(F32)
        for c, span in enumerate(lanes):
            ext[c, pl.ds(HALO + at, chunk_rows), :] = block[:, span]
        return carry

    lax.fori_loop(0, 8, widen, 0)

    swap.wait_recv()
    pan_t[pl.ds(pl.multiple_of(other * half, half), half), :] = pan_ref[other, body, :].T

    def span_of(c):
        return slice(c * wide_c, (c + 1) * wide_c)

    def first_copy(c, step):
        (size, at, peer), (size_s, _, _) = ways[c]
        length = size_s * unit
        src = pl.ds(pl.multiple_of(lax.rem(at + step, size) * length, unit), length)
        return remote(part.at[c, src], got_first.at[c, step, pl.ds(0, length)], ring_sems, (c, 0, step), (peer(step), col))

    def second_copy(c, step):
        _, (size, at, peer) = ways[c]
        src = pl.ds(pl.multiple_of(lax.rem(at + step, size) * unit, unit), unit)
        return remote(middle.at[c, src], got_second.at[c, step], ring_sems, (c, 1, step), (peer(step), col))

    def own_block(c):
        (_, at, _), (size_s, _, _) = ways[c]
        return pl.multiple_of(c * wide_c + at * size_s * unit, unit)

    def third_copy(c, step):
        _, (_, at, peer) = ways[c]
        mine = pl.ds(pl.multiple_of(own_block(c) + at * unit, unit), unit)
        return remote(mix_ref.at[mine], mix_ref.at[mine], ring_sems, (c, 2, step), (peer(step), col))

    def fourth_copy(c, step):
        (_, _, peer), (size_s, _, _) = ways[c]
        mine = pl.ds(own_block(c), size_s * unit)
        return remote(mix_ref.at[mine], mix_ref.at[mine], ring_sems, (c, 3, step), (peer(step), col))

    def first_steps(c):
        return range(1, ways[c][0][0])

    def second_steps(c):
        return range(1, ways[c][1][0])

    def after_first(c):
        (_, at, _), (size_s, _, _) = ways[c]
        length = size_s * unit
        for step in first_steps(c):
            first_copy(c, step).wait_recv()
        total = part[c, pl.ds(pl.multiple_of(at * length, unit), length), :].astype(F32)
        for step in first_steps(c):
            total = total + got_first[c, step, 0:length, :].astype(F32)
        middle[c, 0:length, :] = total.astype(BF16)
        for step in second_steps(c):
            second_copy(c, step).start()

    def after_second(c):
        _, (_, at, _) = ways[c]
        for step in second_steps(c):
            second_copy(c, step).wait_recv()
        inner = middle[c, pl.ds(pl.multiple_of(at * unit, unit), unit), :].astype(F32)
        for step in second_steps(c):
            inner = inner + got_second[c, step].astype(F32)
        top = inner.astype(BF16)
        rest = (inner - top.astype(F32)).astype(BF16)
        both = jnp.dot(jnp.concatenate([top, rest], axis=0), factor_hi[...], preferred_element_type=F32)
        mixed = both[0:unit] + both[unit:] + jnp.dot(top, factor_lo[...], preferred_element_type=F32)
        mix_ref[pl.ds(pl.multiple_of(own_block(c) + at * unit, unit), unit), :] = mixed.astype(BF16)
        for step in second_steps(c):
            third_copy(c, step).start()

    def after_third(c):
        for step in second_steps(c):
            third_copy(c, step).wait_recv()
        for step in first_steps(c):
            fourth_copy(c, step).start()

    def after_fourth(c):
        for step in first_steps(c):
            fourth_copy(c, step).wait_recv()

    for c in range(chunks):
        inner = jnp.dot(pan_t[...], vec[:, span_of(c)], preferred_element_type=F32)
        part[c] = inner.T.astype(BF16)
        for step in first_steps(c):
            first_copy(c, step).start()
    for copy in vec_halos:
        copy.start()

    for which in (0, 1):
        pext[which, HALO:HALO + rows, :] = pan_ref[which, body, :].astype(F32)
    for copy in count_copies:
        copy.wait_recv()
    here = basis_ref[...].astype(F32)
    prev, post = counts[0].astype(F32), counts[1].astype(F32)
    lower = jnp.where(iota(atoms, atoms, 0) < iota(atoms, atoms, 1), 1.0, 0.0).astype(BF16)
    table = jnp.concatenate([prev, here, post, jnp.zeros((5, atoms), F32)], axis=0).astype(BF16)
    first = jnp.dot(table, lower, preferred_element_type=F32).astype(jnp.int32)
    first_ref[...] = jnp.clip(first + (HALO - rows) + rows * iota(8, atoms, 0), 0, rows + 2 * HALO)
    begin_copy = pltpu.make_async_copy(first_ref, starts, start_sem)
    begin_copy.start()
    lines = []
    at = iota(1, atoms, 1)
    for k in range(K):
        d = k - RIM
        near = here
        if d != 0:
            turn = (-d) % atoms
            inside = (at + d >= 0) & (at + d < atoms)
            near = jnp.where(inside, pltpu.roll(here, turn, 1), pltpu.roll(prev if d < 0 else post, turn, 1))
        lines.append(jnp.where(present_ref[k:k + 1, :] > 0, near, 0.0))
    lines.append(proj_ref[...].astype(F32))
    lines.append(jnp.zeros((atoms - K - 1, atoms), F32))
    limit[...] = jnp.concatenate(lines, axis=0).T
    blocks.wait()

    in_i = group_of(GROUP, wide, 1, BMAX, NPMAX)
    slot = (iota(GROUP, wide, 1) - BMAX * in_i).astype(F32)
    in_i = in_i.astype(F32)
    lane = iota(8, 128, 1)

    def band_step(t, carry):
        chunk = pl.ds(pl.multiple_of(t * GROUP, GROUP), GROUP)
        bounds = limit[chunk, :]
        valid = in_i < bounds[:, K:K + 1]
        for k in range(K):
            block = cm_ref[k, chunk, :].astype(F32)
            block = jnp.where(valid & (slot < bounds[:, k:k + 1]), block, 0.0)
            top = (GROUP + K - 2 - k) * GROUP
            for tile in range(wide // 128):
                skew[tile, top:top + GROUP, :] = block[:, tile * 128:(tile + 1) * 128]
        for i in range(NPMAX):
            sides = []
            for side in range(GROUP // 8):
                near = range(8 * side, 8 * side + 8 + K - 1)
                tiles = []
                for tile in range(WIN // 128):
                    acc, end = jnp.zeros((8, 128), F32), 0
                    for b in near:
                        to, last = max(b * BMAX, tile * 128), min((b + 1) * BMAX, (tile + 1) * 128)
                        while to < last:
                            source = i * BMAX + to - b * BMAX
                            count = min(last - to, 128 - source % 128)
                            begin = (REACH - 1 - b) * GROUP + 8 * side * (GROUP + 1)
                            piece = skew[source // 128, pl.ds(begin, 8, stride=GROUP + 1), :]
                            turn = (to - source) % 128
                            piece = piece if turn == 0 else pltpu.roll(piece, turn, 1)
                            acc = jnp.where(lane >= to % 128, piece, acc)
                            to += count
                            end = (to - 1) % 128 + 1
                    tiles.append(jnp.where(lane < end, acc, 0.0) if 0 < end < 128 else acc)
                sides.append(jnp.concatenate(tiles, axis=1))
            band[t, i * GROUP:(i + 1) * GROUP, :] = jnp.concatenate(sides, axis=0).astype(BF16)
        return carry

    def gather(t, carry):
        at = pl.multiple_of(2 * t * BMAX, 16)
        begins = []
        for e in (0, 1):
            flat = 2 * t + e + atoms - RIM
            begins.append(starts[lax.div(flat, atoms), lax.rem(flat, atoms)])
        for c, span in enumerate(lanes):
            both = [ext[c, pl.ds(begin, BMAX), :] for begin in begins]
            padded[pl.ds(at, 2 * BMAX), span] = jnp.concatenate(both, axis=0).astype(BF16)
        for c in (0, 1):
            both = [pext[c, pl.ds(begin, BMAX), :] for begin in begins]
            ppadded[pl.ds(at, 2 * BMAX), c * half:(c + 1) * half] = jnp.concatenate(both, axis=0).astype(BF16)
        return carry

    def project(g, carry):
        at = pl.ds(pl.multiple_of(g * GROUP * BMAX, 16), WIN)
        base[g] = jnp.dot(band[g], padded[at, :], preferred_element_type=F32)
        lean[g] = jnp.dot(band[g], ppadded[at, :], preferred_element_type=F32).astype(BF16)
        return carry

    lax.fori_loop(0, groups // 2, band_step, 0)
    for c in range(chunks):
        after_first(c)
    lax.fori_loop(groups // 2, groups, band_step, 0)
    for c in range(chunks):
        after_second(c)
    begin_copy.wait()
    lax.fori_loop(RIM // 2, (atoms + RIM) // 2, gather, 0)
    for c in range(chunks):
        after_third(c)
    lax.fori_loop(1, groups - 1, project, 0)

    size = GROUP * NPMAX
    same = (iota(size, size, 0) & (GROUP - 1)) == (iota(size, size, 1) & (GROUP - 1))
    expand = jnp.where(group_of(size, size, 0, GROUP, NPMAX) == (iota(size, size, 1) & (NPMAX - 1)), 1.0, 0.0).astype(BF16)
    owner = group_of(GROUP, size, 1, NPMAX, NPMAX)

    def tail(c, g):
        update = lax.dot_general(lean[g], mix_ref[span_of(c), :], across, preferred_element_type=F32)
        rounded = (base[g, :, span_of(c)] - update).astype(BF16)
        weighted = (rounded.astype(F32) * weight[:, span_of(c)]).astype(BF16)
        product = lax.dot_general(weighted, rounded, across, preferred_element_type=F32)
        full[g] = product if c == 0 else full[g] + product

    def finish(g):
        kept = jnp.where(same, full[g], 0.0)
        top = kept.astype(BF16)
        rest = (kept - top.astype(F32)).astype(BF16)
        spread = jnp.dot(top, expand, preferred_element_type=F32) + jnp.dot(rest, expand, preferred_element_type=F32)
        result = jnp.zeros((GROUP, size), F32)
        for i in range(NPMAX):
            result = jnp.where(owner == i, spread[i * GROUP:(i + 1) * GROUP, :], result)
        dens[pl.ds(pl.multiple_of(g * GROUP, GROUP), GROUP), :] = result

    for c in range(chunks):
        after_fourth(c)

        def step_of(g, carry, c=c):
            tail(c, g)
            return carry

        lax.fori_loop(1, groups - 1, step_of, 0)

    def finish_step(g, carry):
        finish(g)
        return carry

    lax.fori_loop(1, groups - 1, finish_step, 0)
    share = own_ref.shape[0]
    inside = share - GROUP

    def den_copy(start, count, slot):
        src = pl.ds(pl.multiple_of(start, GROUP), count)
        dst = pl.ds(pl.multiple_of(start - other * share, GROUP), count)
        return remote(dens.at[src], got_ref.at[dst], den_sems, (slot,), (row, other))

    sent = [den_copy(other * share + GROUP * col, inside, 0), den_copy(other * (atoms - GROUP), GROUP, 1)]
    sent[0].start()

    for copy in pan_halos + vec_halos:
        copy.wait()
    for side, at in ((0, 0), (1, HALO + rows)):
        block = halo_ref[side].astype(F32)
        for c, span in enumerate(lanes):
            ext[c, at:at + HALO, :] = block[:, span]
        for which in (0, 1):
            pext[which, at:at + HALO, :] = pan_ref[which, at:at + HALO, :].astype(F32)
    lax.fori_loop(0, RIM // 2, gather, 0)
    lax.fori_loop((atoms + RIM) // 2, (atoms + 2 * RIM) // 2, gather, 0)

    def last_group(g):
        project(g, 0)
        for c in range(chunks):
            tail(c, g)
        finish(g)

    def last_step(t, carry):
        last_group(lax.rem(other + t, 2) * (groups - 1))

        @pl.when(t == 0)
        def _():
            sent[1].start()

        return carry

    lax.fori_loop(0, 2, last_step, 0)
    own_ref[...] = dens[pl.ds(pl.multiple_of(col * share, share), share), :]

    for copy in sent:
        copy.wait()
    swap.wait_send()
    for copy in count_copies:
        copy.wait_send()
    for c in range(chunks):
        for step in first_steps(c):
            first_copy(c, step).wait_send()
            fourth_copy(c, step).wait_send()
        for step in second_steps(c):
            second_copy(c, step).wait_send()
            third_copy(c, step).wait_send()


def vector_kernel(vin_ref, pan_ref, mix_ref, own_ref, got_ref, vec_ref, den_ref, mixing):
    step = pl.program_id(0)
    tile = vec_ref.shape[0]

    @pl.when(step == 0)
    def _():
        mixing[...] = mix_ref[...].T
        den_ref[...] = own_ref[...] + got_ref[...]

    at = pl.multiple_of(step * tile, 16)
    inside = pl.ds(pl.multiple_of(HALO + at, 16), tile)
    panel = jnp.concatenate([pan_ref[0, inside, :], pan_ref[1, inside, :]], axis=1)
    update = jnp.dot(panel, mixing[...], preferred_element_type=F32)
    vec_ref[...] = (vin_ref[pl.ds(at, tile), :].astype(F32) - update).astype(BF16)


def local(vectors_in, panel, factor, atom_basis, proj_count, coupling, block_present, occ_mask, occ_weight):
    n = lax.axis_size("row")
    rows, cols = vectors_in.shape
    half = panel.shape[1]
    npan = factor.shape[0]
    atoms = atom_basis.shape[1]
    groups = atoms // GROUP
    share = atoms // lax.axis_size("col")
    wide = coupling.shape[2]
    vmem = pl.BlockSpec(memory_space=pltpu.VMEM)
    hbm = pl.BlockSpec(memory_space=pl.ANY)
    plane = max(d for d in range(1, n + 1) if n % d == 0 and d * d <= n)
    most, least = max(plane, n // plane), min(plane, n // plane)
    chunks = max(1, cols // (n * 16))
    width = cols // chunks
    unit = width // n
    ext_rows = rows + 2 * HALO
    pad_rows = (groups - 1) * GROUP * BMAX + WIN
    dma = pltpu.SemaphoreType.DMA
    operands = (vectors_in, panel, jnp.swapaxes(coupling, 0, 1), factor, atom_basis, proj_count[None, :], block_present.T)
    operands = [pltpu.with_memory_space_constraint(x, pltpu.HBM) for x in operands]
    vin, pan, mix, own, got = pl.pallas_call(
        functools.partial(mix_kernel, n, plane),
        out_shape=(
            jax.ShapeDtypeStruct((rows, cols), BF16),
            jax.ShapeDtypeStruct((2, ext_rows, half), BF16),
            jax.ShapeDtypeStruct((cols, npan), BF16),
            jax.ShapeDtypeStruct((share, NPMAX * NPMAX), F32),
            jax.ShapeDtypeStruct((share, NPMAX * NPMAX), F32),
        ),
        in_specs=[hbm] * 3 + [vmem] * 6,
        out_specs=(vmem,) * 5,
        scratch_shapes=[
            pltpu.VMEM((npan, rows), BF16),
            pltpu.VMEM((chunks, width, npan), BF16),
            pltpu.VMEM((chunks, most, width // least, npan), BF16),
            pltpu.VMEM((chunks, width // least, npan), BF16),
            pltpu.VMEM((chunks, most, unit, npan), BF16),
            pltpu.VMEM((npan, npan), BF16),
            pltpu.VMEM((npan, npan), BF16),
            pltpu.VMEM((2, 1, atoms), jnp.int32),
            pltpu.VMEM((atoms, atoms), F32),
            pltpu.VMEM((K, atoms, wide), BF16),
            pltpu.VMEM((2, HALO, cols), BF16),
            pltpu.VMEM((wide // 128, (2 * GROUP + K - 2) * GROUP, 128), F32),
            pltpu.VMEM((groups, GROUP * NPMAX, WIN), BF16),
            pltpu.VMEM((8, atoms), jnp.int32),
            pltpu.SMEM((8, atoms), jnp.int32),
            pltpu.VMEM((cols // 128, ext_rows + BMAX, 128), F32),
            pltpu.VMEM((2, ext_rows + BMAX, half), F32),
            pltpu.VMEM((pad_rows, cols), BF16),
            pltpu.VMEM((pad_rows, npan), BF16),
            pltpu.VMEM((groups, GROUP * NPMAX, cols), F32),
            pltpu.VMEM((groups, GROUP * NPMAX, npan), BF16),
            pltpu.VMEM((groups, GROUP * NPMAX, GROUP * NPMAX), F32),
            pltpu.VMEM((atoms, NPMAX * NPMAX), F32),
            pltpu.VMEM((1, cols), F32),
            dma((2,)), dma, dma, dma, dma((2, 5)), dma((2, 2)), dma((2, 2)),
            dma((2, chunks, 4, most)), dma((2, 2)),
        ],
        compiler_params=pltpu.CompilerParams(collective_id=0, has_side_effects=True, vmem_limit_bytes=48 << 20),
        cost_estimate=pl.CostEstimate(flops=8 * 10**9, bytes_accessed=10 << 20, transcendentals=0),
    )(*operands, occ_mask[None, :], occ_weight[None, :])

    tile = rows // 8
    return pl.pallas_call(
        vector_kernel,
        out_shape=(
            jax.ShapeDtypeStruct((rows, cols), BF16),
            jax.ShapeDtypeStruct((share, NPMAX * NPMAX), F32),
        ),
        grid=(rows // tile,),
        in_specs=[vmem] * 5,
        out_specs=[
            pl.BlockSpec((tile, cols), lambda s: (s, 0)),
            pl.BlockSpec((share, NPMAX * NPMAX), lambda s: (0, 0)),
        ],
        scratch_shapes=[pltpu.VMEM((npan, cols), BF16)],
        compiler_params=pltpu.CompilerParams(vmem_limit_bytes=16 << 20),
        cost_estimate=pl.CostEstimate(flops=6 * 10**9, bytes_accessed=10 << 20, transcendentals=0),
    )(vin, pan, mix, own, got)


def solution(mesh):
    placed = (
        P("row", "col"),
        P("row", "col"),
        P(),
        P("row", None),
        P("row"),
        P("row", None, None),
        P("row", None),
        P("col"),
        P("col"),
    )
    return jax.shard_map(
        local,
        mesh=mesh,
        in_specs=placed,
        out_specs=(P("row", "col"), P(("row", "col"), None)),
        check_vma=False,
    )
```

time: 49.8 us -> 58.6 us (1.18)
  Pallas kernels: 46.9 us -> 56.3 us
  local copies, waits for them, and re-layouts: 0.01 us -> 1.37 us
  waiting for transfers between devices: 1.24 us -> 0 us
  other arithmetic: 0.64 us -> 0 us
    pallas_call x1, Pallas kernels: 37.2 us -> 51.4 us  [local(): pl.pallas_call(functools.partial(mix_kernel, n, plane), out_shape=(jax.Sh...]
    pallas_call x1, Pallas kernels: 9.67 us -> 4.93 us  [local(): pl.pallas_call(vector_kernel, out_shape=(jax.ShapeDtypeStruct((rows, cols...]
    unnamed x4, local copies, waits for them, and re-layouts: 0.01 us -> 1.37 us
    ppermute x1 -> x0, waiting for transfers between devices: 1.24 us -> none  [local(): lax.ppermute(sent, 'col', [(i, (i + step) % ncol) for i in range(ncol)])]
    add x1 -> x0, other arithmetic: 0.64 us -> none  [local(): density + lax.ppermute(sent, 'col', [(i, (i + step) % ncol) for i in rang...]
  transfers between devices with their start and end apart: 1 -> 0, of which waited for: 1 -> 0; matrix products, arithmetic and copies ran while one was open for 0% -> 0% of each run, Pallas kernels for 0% -> 0%
where the time goes in v1:
time: 58.6 us; the launch traced here: 58.3 us
  Pallas kernels  56.3 us (96%)
  local copies, waits for them, and re-layouts  1.37 us (2%)
  between operations  0.65 us (1%)
    pallas_call x1, Pallas kernels, local(): pl.pallas_call(functools.partial(mix_kernel, n, plane), out_shape=(jax.Sh...  51.4 us
    pallas_call x1, Pallas kernels, local(): pl.pallas_call(vector_kernel, out_shape=(jax.ShapeDtypeStruct((rows, cols...  4.93 us
    unnamed x4, local copies, waits for them, and re-layouts  1.37 us

profile of v1, /device:TPU:0, one launch (start us, length us, event | category | flops | bytes accessed | tf_op | source)
XLA Modules:
  0.0 58.3 jit_solution(14193449111227058555)
XLA Ops:
  0.6 0.0 copy-start
  0.6 0.7 %copy-done = s32[1024]{0:T(1024)S(1)} copy-done((s32[1024]{0:T(1024)S(1)}, s32[1024]{0:T(1024)}, u32[]{:S(2)}) %copy-start) | copy-done | bytes 4120
  1.3 0.0 copy-start.1
  1.3 0.7 %copy-done.1 = f32[1024]{0:T(1024)S(1)} copy-done((f32[1024]{0:T(1024)S(1)}, f32[1024]{0:T(1024)}, u32[]{:S(2)}) %copy-start.1) | copy-done | bytes 4120
  2.0 51.4 %shard_map.104 = (bf16[2048,1024]{1,0:T(8,128)(2,1)S(1)}, bf16[2,2240,128]{2,1,0:T(8,128)(2,1)S(1)}, bf16[1024,256]{1,0:T(8,128)(2,1)S(1)}, f32[64,256]{1,0:T(8,128)S(1)}, f32[64,256]{1,0:T(8,128)S(1)}) custom-call(bf16[2048,1024]{1,0:T(8,128)(2,1)} %vec_hbm.1, bf16[2048,128]{1,0:T(8,128)(2,1)} %panel_hbm.1, bf16[9,128,384]{2,1,0:T(8,128)(2,1)} %bitcast.7, ...), custom_call_target="tpu_custom_call" | custom-call | flops 8000000000 | bytes 10485760 | tf_op jit(solution)/shard_map/pallas_call | solution.py:444
  53.4 4.9 %shard_map.105 = (bf16[2048,1024]{1,0:T(8,128)(2,1)}, f32[64,256]{1,0:T(8,128)}) custom-call(bf16[2048,1024]{1,0:T(8,128)(2,1)S(1)} %get-tuple-element.7.vin_ref, bf16[2,2240,128]{2,1,0:T(8,128)(2,1)S(1)} %get-tuple-element.8.pan_ref, bf16[1024,256]{1,0:T(8,128)(2,1)S(1)} %get-tuple-element.9.mix_ref, f32[64,256]{1,0:T(8,128)S(1)} %get-tuple-element.10.own_ref, ...), custom_call_target="tpu_custom_call" | custom-call | flops 6000000000 | bytes 10485760 | tf_op jit(solution)/shard_map/pallas_call | solution.py:488
Async XLA Ops:
  0.6 0.7 %copy-start = (s32[1024]{0:T(1024)S(1)}, s32[1024]{0:T(1024)}, u32[]{:S(2)}) copy-start(s32[1024]{0:T(1024)} %param.16) | copy-start | bytes 12292
  1.3 0.7 %copy-start.1 = (f32[1024]{0:T(1024)S(1)}, f32[1024]{0:T(1024)}, u32[]{:S(2)}) copy-start(f32[1024]{0:T(1024)} %param.17) | copy-start | bytes 12292

commit v2 on v1

--- a/solution.py
+++ b/solution.py
@@ -12,6 +12,7 @@
 K = 9
 RIM = (K - 1) // 2
 HALO = RIM * BMAX
+PIECES = 3
 GROUP = 16
 WIN = -(-(GROUP + K - 1) * BMAX // 128) * 128
 REACH = GROUP + K - 1
@@ -33,11 +34,12 @@
     return jnp.tile(group, (rows // small[0], columns // small[1]))
 
 
-def mix_kernel(n, plane, vec_hbm, panel_hbm, coupling_hbm, factor_ref, basis_ref, proj_ref, present_ref, mask_ref, occ_ref,
+def mix_kernel(n, plane, vec_hbm, panel_hbm, coupling_hbm, factor_hbm, basis_hbm, proj_hbm, present_hbm, mask_hbm, occ_hbm,
                vec, pan_ref, mix_ref, own_ref, got_ref,
+               factor_ref, basis_ref, proj_ref, present_ref, mask_ref, occ_ref,
                pan_t, part, got_first, middle, got_second, factor_hi, factor_lo, counts, limit, cm_ref, halo_ref, skew, band,
                first_ref, starts, ext, pext, padded, ppadded, base, lean, full, dens, weight,
-               load_sem, own_sem, cm_sem, start_sem, pan_sems, halo_sems, count_sems, ring_sems, den_sems):
+               load_sem, small_sem, own_sem, cm_sem, start_sem, pan_sems, halo_sems, count_sems, ring_sems, fold_sems, den_sems):
     row, col = lax.axis_index("row"), lax.axis_index("col")
     other = 1 - col
     up, down = lax.rem(row + 1, n), lax.rem(row + n - 1, n)
@@ -59,7 +61,7 @@
         return lax.rem(line + step, q) * p + spot
 
     by_plane, by_line = (p, spot, plane_peer), (q, line, line_peer)
-    ways = [(by_line, by_plane) if chunks > 2 and c == 0 else (by_plane, by_line) for c in range(chunks)]
+    ways = [(by_line, by_plane) if chunks == 4 and c == 2 else (by_plane, by_line) for c in range(chunks)]
 
     own = pltpu.make_async_copy(panel_hbm, pan_ref.at[col, body], own_sem)
     own.start()
@@ -68,6 +70,11 @@
              for i in range(load_sem.shape[0])]
     for load in loads:
         load.start()
+    small = [pltpu.make_async_copy(src, dst, small_sem.at[i]) for i, (src, dst) in enumerate((
+        (basis_hbm, basis_ref), (factor_hbm, factor_ref), (proj_hbm, proj_ref), (present_hbm, present_ref),
+        (mask_hbm, mask_ref), (occ_hbm, occ_ref)))]
+    for load in small:
+        load.start()
     blocks = pltpu.make_async_copy(coupling_hbm, cm_ref, cm_sem)
     blocks.start()
 
@@ -76,10 +83,6 @@
     greeted += [(up, col), (down, col)] + [(peer, other) for peer in (row, up, down)]
     for target in greeted:
         pl.semaphore_signal(barrier, inc=1, device_id=target, device_id_type=MESH)
-    high = factor_ref[...].astype(BF16)
-    factor_hi[...] = high
-    factor_lo[...] = (factor_ref[...] - high.astype(F32)).astype(BF16)
-    weight[...] = mask_ref[...].astype(F32) * occ_ref[...] / (vec_hbm.shape[1] * lax.axis_size("col"))
     length = ext.shape[1]
     edge = rows + HALO
     ext[:, edge:, :] = jnp.zeros((ext.shape[0], length - edge, 128), F32)
@@ -100,7 +103,7 @@
     swap = remote(panel_hbm, pan_ref.at[col, body], pan_sems, (0,), (row, other))
     swap.start()
     count_copies = [
-        remote(basis_ref, counts.at[side], count_sems, (side,), (target, col))
+        remote(basis_hbm, counts.at[side], count_sems, (side,), (target, col))
         for side, target in ((0, up), (1, down))
     ]
     for copy in count_copies:
@@ -113,12 +116,21 @@
             to = col if where == 0 else other
             pan_halos.append(remote(panel_hbm.at[pl.ds(src_at, HALO)], pan_ref.at[col, pl.ds(dst_at, HALO)],
                                     pan_sems, (1 + 2 * side + where,), (target, to)))
-        vec_halos.append(remote(vec_hbm.at[pl.ds(src_at, HALO)], halo_ref.at[side], halo_sems, (side,), (target, col)))
+        for piece in range(PIECES):
+            part_at = piece * (HALO // PIECES)
+            vec_halos.append(remote(vec_hbm.at[pl.ds(src_at + part_at, HALO // PIECES)],
+                                    halo_ref.at[side, pl.ds(part_at, HALO // PIECES)], halo_sems, (side, piece), (target, col)))
     for copy in pan_halos:
         copy.start()
 
     own.wait()
     pan_t[pl.ds(pl.multiple_of(col * half, half), half), :] = pan_ref[col, body, :].T
+    for load in small:
+        load.wait()
+    high = factor_ref[...].astype(BF16)
+    factor_hi[...] = high
+    factor_lo[...] = (factor_ref[...] - high.astype(F32)).astype(BF16)
+    weight[...] = mask_ref[...].astype(F32) * occ_ref[...] / (vec_hbm.shape[1] * lax.axis_size("col"))
     for load in loads:
         load.wait()
 
@@ -146,30 +158,29 @@
         src = pl.ds(pl.multiple_of(lax.rem(at + step, size) * length, unit), length)
         return remote(part.at[c, src], got_first.at[c, step, pl.ds(0, length)], ring_sems, (c, 0, step), (peer(step), col))
 
-    def second_copy(c, step):
+    def rounds(c):
+        return range(ways[c][1][0].bit_length() - 1)
+
+    def fold_copy(c, turn):
         _, (size, at, peer) = ways[c]
-        src = pl.ds(pl.multiple_of(lax.rem(at + step, size) * unit, unit), unit)
-        return remote(middle.at[c, src], got_second.at[c, step], ring_sems, (c, 1, step), (peer(step), col))
+        reach = 1 << turn
+        ahead = lax.rem(lax.div(at, reach), 2)
+        step = reach + ahead * (size - 2 * reach)
+        length = size * unit
+        return remote(middle.at[c, turn, pl.ds(0, length)], got_second.at[c, turn, pl.ds(0, length)],
+                      fold_sems, (c, turn), (peer(step), col))
 
     def own_block(c):
         (_, at, _), (size_s, _, _) = ways[c]
         return pl.multiple_of(c * wide_c + at * size_s * unit, unit)
 
-    def third_copy(c, step):
-        _, (_, at, peer) = ways[c]
-        mine = pl.ds(pl.multiple_of(own_block(c) + at * unit, unit), unit)
-        return remote(mix_ref.at[mine], mix_ref.at[mine], ring_sems, (c, 2, step), (peer(step), col))
-
-    def fourth_copy(c, step):
+    def last_copy(c, step):
         (_, _, peer), (size_s, _, _) = ways[c]
         mine = pl.ds(own_block(c), size_s * unit)
-        return remote(mix_ref.at[mine], mix_ref.at[mine], ring_sems, (c, 3, step), (peer(step), col))
+        return remote(mix_ref.at[mine], mix_ref.at[mine], ring_sems, (c, 1, step), (peer(step), col))
 
     def first_steps(c):
         return range(1, ways[c][0][0])
-
-    def second_steps(c):
-        return range(1, ways[c][1][0])
 
     def after_first(c):
         (_, at, _), (size_s, _, _) = ways[c]
@@ -179,42 +190,42 @@
         total = part[c, pl.ds(pl.multiple_of(at * length, unit), length), :].astype(F32)
         for step in first_steps(c):
             total = total + got_first[c, step, 0:length, :].astype(F32)
-        middle[c, 0:length, :] = total.astype(BF16)
-        for step in second_steps(c):
-            second_copy(c, step).start()
-
-    def after_second(c):
-        _, (_, at, _) = ways[c]
-        for step in second_steps(c):
-            second_copy(c, step).wait_recv()
-        inner = middle[c, pl.ds(pl.multiple_of(at * unit, unit), unit), :].astype(F32)
-        for step in second_steps(c):
-            inner = inner + got_second[c, step].astype(F32)
+        middle[c, 0, 0:length, :] = total.astype(BF16)
+        fold_copy(c, 0).start()
+
+    def after_fold(c, turn):
+        length = ways[c][1][0] * unit
+        fold_copy(c, turn).wait_recv()
+        inner = middle[c, turn, 0:length, :].astype(F32) + got_second[c, turn, 0:length, :].astype(F32)
         top = inner.astype(BF16)
+        if turn + 1 < len(rounds(c)):
+            middle[c, turn + 1, 0:length, :] = top
+            fold_copy(c, turn + 1).start()
+            return
         rest = (inner - top.astype(F32)).astype(BF16)
         both = jnp.dot(jnp.concatenate([top, rest], axis=0), factor_hi[...], preferred_element_type=F32)
-        mixed = both[0:unit] + both[unit:] + jnp.dot(top, factor_lo[...], preferred_element_type=F32)
-        mix_ref[pl.ds(pl.multiple_of(own_block(c) + at * unit, unit), unit), :] = mixed.astype(BF16)
-        for step in second_steps(c):
-            third_copy(c, step).start()
-
-    def after_third(c):
-        for step in second_steps(c):
-            third_copy(c, step).wait_recv()
+        mixed = both[0:length] + both[length:] + jnp.dot(top, factor_lo[...], preferred_element_type=F32)
+        mix_ref[pl.ds(own_block(c), length), :] = mixed.astype(BF16)
         for step in first_steps(c):
-            fourth_copy(c, step).start()
-
-    def after_fourth(c):
+            last_copy(c, step).start()
+
+    def after_last(c):
         for step in first_steps(c):
-            fourth_copy(c, step).wait_recv()
-
-    for c in range(chunks):
-        inner = jnp.dot(pan_t[...], vec[:, span_of(c)], preferred_element_type=F32)
-        part[c] = inner.T.astype(BF16)
-        for step in first_steps(c):
-            first_copy(c, step).start()
-    for copy in vec_halos:
-        copy.start()
+            last_copy(c, step).wait_recv()
+
+    def start_halos(*which):
+        for piece in which:
+            for copy in vec_halos[piece::PIECES]:
+                copy.start()
+
+    for first_c, last_c in ([(1, 3), (0, 1), (3, 4)] if chunks == 4 else [(0, chunks)]):
+        at = first_c * wide_c
+        inner = jnp.dot(pan_t[...], vec[:, at:last_c * wide_c], preferred_element_type=F32).T.astype(BF16)
+        for c in range(first_c, last_c):
+            part[c] = inner[c * wide_c - at:(c + 1) * wide_c - at]
+            for step in first_steps(c):
+                first_copy(c, step).start()
+    start_halos(0)
 
     for which in (0, 1):
         pext[which, HALO:HALO + rows, :] = pan_ref[which, body, :].astype(F32)
@@ -302,32 +313,60 @@
         lean[g] = jnp.dot(band[g], ppadded[at, :], preferred_element_type=F32).astype(BF16)
         return carry
 
-    lax.fori_loop(0, groups // 2, band_step, 0)
-    for c in range(chunks):
-        after_first(c)
-    lax.fori_loop(groups // 2, groups, band_step, 0)
-    for c in range(chunks):
-        after_second(c)
+    def bands(low, high):
+        lax.fori_loop(low, high, band_step, 0)
+
+    def gathers(low, high):
+        lax.fori_loop(low, high, gather, 0)
+
+    def projects(low, high):
+        lax.fori_loop(low, high, project, 0)
+
     begin_copy.wait()
-    lax.fori_loop(RIM // 2, (atoms + RIM) // 2, gather, 0)
-    for c in range(chunks):
-        after_third(c)
-    lax.fori_loop(1, groups - 1, project, 0)
+    inside_from, inside_to = RIM // 2, (atoms + RIM) // 2
+    inside_mid = (inside_from + inside_to) // 2
+    eighth = groups // 4
+    works = [functools.partial(bands, t * eighth, (t + 1) * eighth) for t in range(4)]
+    works += [functools.partial(gathers, inside_from, inside_mid), functools.partial(gathers, inside_mid, inside_to)]
+    works += [functools.partial(projects, g, g + 1) for g in range(1, groups - 1)]
+    if chunks == 4:
+        order = [
+            [],
+            [(after_first, 1)],
+            [(after_first, 0)],
+            [(after_fold, 1, 0)],
+            [(after_first, 2), (after_first, 3), (after_fold, 0, 0)],
+            [],
+            [(after_fold, 2, 0), (after_fold, 1, 1), (after_fold, 3, 0)],
+            [],
+            [(after_fold, 0, 1), (after_fold, 2, 1)],
+            [],
+            [(after_fold, 3, 1), (start_halos, 1, 2)],
+            [],
+        ]
+    else:
+        every = range(chunks)
+        order = [[], [(after_first, c) for c in every] + [(start_halos, 1, 2)]]
+        order += [[(after_fold, c, turn) for c in every] for turn in range(len(rounds(0)))]
+        order += [[] for _ in works[len(order):]]
+    for work, events in zip(works, order, strict=True):
+        work()
+        for event in events:
+            event[0](*event[1:])
 
     size = GROUP * NPMAX
     same = (iota(size, size, 0) & (GROUP - 1)) == (iota(size, size, 1) & (GROUP - 1))
     expand = jnp.where(group_of(size, size, 0, GROUP, NPMAX) == (iota(size, size, 1) & (NPMAX - 1)), 1.0, 0.0).astype(BF16)
     owner = group_of(GROUP, size, 1, NPMAX, NPMAX)
 
-    def tail(c, g):
-        update = lax.dot_general(lean[g], mix_ref[span_of(c), :], across, preferred_element_type=F32)
-        rounded = (base[g, :, span_of(c)] - update).astype(BF16)
-        weighted = (rounded.astype(F32) * weight[:, span_of(c)]).astype(BF16)
-        product = lax.dot_general(weighted, rounded, across, preferred_element_type=F32)
-        full[g] = product if c == 0 else full[g] + product
-
-    def finish(g):
-        kept = jnp.where(same, full[g], 0.0)
+    def tail(span, g):
+        update = lax.dot_general(lean[g], mix_ref[span, :], across, preferred_element_type=F32)
+        rounded = (base[g, :, span] - update).astype(BF16)
+        weighted = (rounded.astype(F32) * weight[:, span]).astype(BF16)
+        return lax.dot_general(weighted, rounded, across, preferred_element_type=F32)
+
+    def finish(product, g):
+        kept = jnp.where(same, product, 0.0)
         top = kept.astype(BF16)
         rest = (kept - top.astype(F32)).astype(BF16)
         spread = jnp.dot(top, expand, preferred_element_type=F32) + jnp.dot(rest, expand, preferred_element_type=F32)
@@ -336,20 +375,28 @@
             result = jnp.where(owner == i, spread[i * GROUP:(i + 1) * GROUP, :], result)
         dens[pl.ds(pl.multiple_of(g * GROUP, GROUP), GROUP), :] = result
 
-    for c in range(chunks):
-        after_fourth(c)
-
-        def step_of(g, carry, c=c):
-            tail(c, g)
-            return carry
-
-        lax.fori_loop(1, groups - 1, step_of, 0)
-
-    def finish_step(g, carry):
-        finish(g)
+    cut = vec.shape[1] // 2
+    first_half, second_half = slice(0, cut), slice(cut, 2 * cut)
+    batch = max(d for d in (3, 2, 1) if (groups - 2) % d == 0)
+
+    def tail_first(t, carry):
+        for e in range(batch):
+            g = 1 + t * batch + e
+            full[g] = tail(first_half, g)
         return carry
 
-    lax.fori_loop(1, groups - 1, finish_step, 0)
+    def tail_second(t, carry):
+        products = [full[1 + t * batch + e] + tail(second_half, 1 + t * batch + e) for e in range(batch)]
+        for e, product in enumerate(products):
+            finish(product, 1 + t * batch + e)
+        return carry
+
+    for c in range(0, max(1, chunks // 2)):
+        after_last(c)
+    lax.fori_loop(0, (groups - 2) // batch, tail_first, 0)
+    for c in range(max(1, chunks // 2), chunks):
+        after_last(c)
+    lax.fori_loop(0, (groups - 2) // batch, tail_second, 0)
     share = own_ref.shape[0]
     inside = share - GROUP
 
@@ -372,22 +419,14 @@
     lax.fori_loop(0, RIM // 2, gather, 0)
     lax.fori_loop((atoms + RIM) // 2, (atoms + 2 * RIM) // 2, gather, 0)
 
-    def last_group(g):
-        project(g, 0)
-        for c in range(chunks):
-            tail(c, g)
-        finish(g)
-
-    def last_step(t, carry):
-        last_group(lax.rem(other + t, 2) * (groups - 1))
-
-        @pl.when(t == 0)
-        def _():
-            sent[1].start()
-
-        return carry
-
-    lax.fori_loop(0, 2, last_step, 0)
+    every = slice(0, 2 * cut)
+    theirs, ours = other * (groups - 1), col * (groups - 1)
+    project(theirs, 0)
+    product = tail(every, theirs)
+    project(ours, 0)
+    finish(product, theirs)
+    sent[1].start()
+    finish(tail(every, ours), ours)
     own_ref[...] = dens[pl.ds(pl.multiple_of(col * share, share), share), :]
 
     for copy in sent:
@@ -398,26 +437,26 @@
     for c in range(chunks):
         for step in first_steps(c):
             first_copy(c, step).wait_send()
-            fourth_copy(c, step).wait_send()
-        for step in second_steps(c):
-            second_copy(c, step).wait_send()
-            third_copy(c, step).wait_send()
-
-
-def vector_kernel(vin_ref, pan_ref, mix_ref, own_ref, got_ref, vec_ref, den_ref, mixing):
-    step = pl.program_id(0)
-    tile = vec_ref.shape[0]
-
-    @pl.when(step == 0)
-    def _():
-        mixing[...] = mix_ref[...].T
-        den_ref[...] = own_ref[...] + got_ref[...]
-
-    at = pl.multiple_of(step * tile, 16)
-    inside = pl.ds(pl.multiple_of(HALO + at, 16), tile)
-    panel = jnp.concatenate([pan_ref[0, inside, :], pan_ref[1, inside, :]], axis=1)
-    update = jnp.dot(panel, mixing[...], preferred_element_type=F32)
-    vec_ref[...] = (vin_ref[pl.ds(at, tile), :].astype(F32) - update).astype(BF16)
+            last_copy(c, step).wait_send()
+        for turn in rounds(c):
+            fold_copy(c, turn).wait_send()
+
+
+def vector_kernel(vin_ref, pan_ref, mix_ref, own_ref, got_ref, vec_hbm, den_ref, done, sems):
+    tiles = sems.shape[0]
+    tile = vin_ref.shape[0] // tiles
+    den_ref[...] = own_ref[...] + got_ref[...]
+    copies = []
+    for t in range(tiles):
+        at = slice(t * tile, (t + 1) * tile)
+        inside = slice(HALO + t * tile, HALO + (t + 1) * tile)
+        panel = jnp.concatenate([pan_ref[0, inside, :], pan_ref[1, inside, :]], axis=1)
+        update = lax.dot_general(panel, mix_ref[...], (((1,), (1,)), ((), ())), preferred_element_type=F32)
+        done[at, :] = (vin_ref[at, :].astype(F32) - update).astype(BF16)
+        copies.append(pltpu.make_async_copy(done.at[at], vec_hbm.at[at], sems.at[t]))
+        copies[-1].start()
+    for copy in copies:
+        copy.wait()
 
 
 def local(vectors_in, panel, factor, atom_basis, proj_count, coupling, block_present, occ_mask, occ_weight):
@@ -436,10 +475,12 @@
     chunks = max(1, cols // (n * 16))
     width = cols // chunks
     unit = width // n
+    turns = most.bit_length() - 1
     ext_rows = rows + 2 * HALO
     pad_rows = (groups - 1) * GROUP * BMAX + WIN
     dma = pltpu.SemaphoreType.DMA
-    operands = (vectors_in, panel, jnp.swapaxes(coupling, 0, 1), factor, atom_basis, proj_count[None, :], block_present.T)
+    operands = (vectors_in, panel, jnp.swapaxes(coupling, 0, 1), factor, atom_basis, proj_count[None, :], block_present.T,
+                occ_mask[None, :], occ_weight[None, :])
     operands = [pltpu.with_memory_space_constraint(x, pltpu.HBM) for x in operands]
     vin, pan, mix, own, got = pl.pallas_call(
         functools.partial(mix_kernel, n, plane),
@@ -450,14 +491,15 @@
             jax.ShapeDtypeStruct((share, NPMAX * NPMAX), F32),
             jax.ShapeDtypeStruct((share, NPMAX * NPMAX), F32),
         ),
-        in_specs=[hbm] * 3 + [vmem] * 6,
+        in_specs=[hbm] * 9,
         out_specs=(vmem,) * 5,
         scratch_shapes=[
+            *[pltpu.VMEM(x.shape, x.dtype) for x in operands[3:]],
             pltpu.VMEM((npan, rows), BF16),
             pltpu.VMEM((chunks, width, npan), BF16),
             pltpu.VMEM((chunks, most, width // least, npan), BF16),
-            pltpu.VMEM((chunks, width // least, npan), BF16),
-            pltpu.VMEM((chunks, most, unit, npan), BF16),
+            pltpu.VMEM((chunks, turns, width // least, npan), BF16),
+            pltpu.VMEM((chunks, turns, width // least, npan), BF16),
             pltpu.VMEM((npan, npan), BF16),
             pltpu.VMEM((npan, npan), BF16),
             pltpu.VMEM((2, 1, atoms), jnp.int32),
@@ -477,27 +519,22 @@
             pltpu.VMEM((groups, GROUP * NPMAX, GROUP * NPMAX), F32),
             pltpu.VMEM((atoms, NPMAX * NPMAX), F32),
             pltpu.VMEM((1, cols), F32),
-            dma((2,)), dma, dma, dma, dma((2, 5)), dma((2, 2)), dma((2, 2)),
-            dma((2, chunks, 4, most)), dma((2, 2)),
+            dma((2,)), dma((6,)), dma, dma, dma, dma((2, 5)), dma((2, 2, PIECES)), dma((2, 2)),
+            dma((2, chunks, 2, most)), dma((2, chunks, turns)), dma((2, 2)),
         ],
         compiler_params=pltpu.CompilerParams(collective_id=0, has_side_effects=True, vmem_limit_bytes=48 << 20),
         cost_estimate=pl.CostEstimate(flops=8 * 10**9, bytes_accessed=10 << 20, transcendentals=0),
-    )(*operands, occ_mask[None, :], occ_weight[None, :])
-
-    tile = rows // 8
+    )(*operands)
+
     return pl.pallas_call(
         vector_kernel,
         out_shape=(
             jax.ShapeDtypeStruct((rows, cols), BF16),
             jax.ShapeDtypeStruct((share, NPMAX * NPMAX), F32),
         ),
-        grid=(rows // tile,),
         in_specs=[vmem] * 5,
-        out_specs=[
-            pl.BlockSpec((tile, cols), lambda s: (s, 0)),
-            pl.BlockSpec((share, NPMAX * NPMAX), lambda s: (0, 0)),
-        ],
-        scratch_shapes=[pltpu.VMEM((npan, cols), BF16)],
+        out_specs=[hbm, vmem],
+        scratch_shapes=[pltpu.VMEM((rows, cols), BF16), dma((8,))],
         compiler_params=pltpu.CompilerParams(vmem_limit_bytes=16 << 20),
         cost_estimate=pl.CostEstimate(flops=6 * 10**9, bytes_accessed=10 << 20, transcendentals=0),
     )(vin, pan, mix, own, got)

time: 58.6 us -> 40.5 us (0.69)
  Pallas kernels: 56.3 us -> 39.7 us
  local copies, waits for them, and re-layouts: 1.37 us -> 0 us
    pallas_call x1, Pallas kernels: 51.4 us -> 36.7 us  [local(): pl.pallas_call(functools.partial(mix_kernel, n, plane), out_shape=(jax.Sh...]
    pallas_call x1, Pallas kernels: 4.93 us -> 3.04 us  [local(): pl.pallas_call(vector_kernel, out_shape=(jax.ShapeDtypeStruct((rows, cols...]
    unnamed x4 -> x0, local copies, waits for them, and re-layouts: 1.37 us -> none
where the time goes in v2:
time: 40.5 us; the launch traced here: 40.3 us
  Pallas kernels  39.7 us (98%)
  between operations  0.64 us (2%)
    pallas_call x1, Pallas kernels, local(): pl.pallas_call(functools.partial(mix_kernel, n, plane), out_shape=(jax.Sh...  36.7 us
    pallas_call x1, Pallas kernels, local(): pl.pallas_call(vector_kernel, out_shape=(jax.ShapeDtypeStruct((rows, cols...  3.04 us

profile of v2, /device:TPU:0, one launch (start us, length us, event | category | flops | bytes accessed | tf_op | source)
XLA Modules:
  0.0 40.3 jit_solution(5634563746814405922)
XLA Ops:
  0.6 36.7 %shard_map.104 = (bf16[2048,1024]{1,0:T(8,128)(2,1)S(1)}, bf16[2,2240,128]{2,1,0:T(8,128)(2,1)S(1)}, bf16[1024,256]{1,0:T(8,128)(2,1)S(1)}, f32[64,256]{1,0:T(8,128)S(1)}, f32[64,256]{1,0:T(8,128)S(1)}) custom-call(bf16[2048,1024]{1,0:T(8,128)(2,1)} %vec_hbm.1, bf16[2048,128]{1,0:T(8,128)(2,1)} %panel_hbm.1, bf16[9,128,384]{2,1,0:T(8,128)(2,1)} %bitcast.5, ...), custom_call_target="tpu_custom_call" | custom-call | flops 8000000000 | bytes 10485760 | tf_op jit(solution)/shard_map/pallas_call | solution.py:485
  37.3 3.0 %shard_map.105 = (bf16[2048,1024]{1,0:T(8,128)(2,1)}, f32[64,256]{1,0:T(8,128)}) custom-call(bf16[2048,1024]{1,0:T(8,128)(2,1)S(1)} %get-tuple-element.7.vin_ref, bf16[2,2240,128]{2,1,0:T(8,128)(2,1)S(1)} %get-tuple-element.8.pan_ref, bf16[1024,256]{1,0:T(8,128)(2,1)S(1)} %get-tuple-element.9.mix_ref, f32[64,256]{1,0:T(8,128)S(1)} %get-tuple-element.10.own_ref, ...), custom_call_target="tpu_custom_call" | custom-call | flops 6000000000 | bytes 10485760 | tf_op jit(solution)/shard_map/pallas_call | solution.py:529

commit v3 on v2

--- a/solution.py
+++ b/solution.py
@@ -12,10 +12,11 @@
 K = 9
 RIM = (K - 1) // 2
 HALO = RIM * BMAX
-PIECES = 3
+PIECES = 6
 GROUP = 16
-WIN = -(-(GROUP + K - 1) * BMAX // 128) * 128
-REACH = GROUP + K - 1
+SUB = 8
+WIN = -(-(SUB + K - 1) * BMAX // 128) * 128
+REACH = SUB + K - 1
 F32 = jnp.float32
 BF16 = jnp.bfloat16
 MESH = pl.DeviceIdType.MESH
@@ -76,23 +77,19 @@
     for load in small:
         load.start()
     blocks = pltpu.make_async_copy(coupling_hbm, cm_ref, cm_sem)
-    blocks.start()
 
     barrier = pltpu.get_barrier_semaphore()
     greeted = [(plane_peer(step), col) for step in range(1, p)] + [(line_peer(step), col) for step in range(1, q)]
-    greeted += [(up, col), (down, col)] + [(peer, other) for peer in (row, up, down)]
+    greeted += [(row, other)]
     for target in greeted:
         pl.semaphore_signal(barrier, inc=1, device_id=target, device_id_type=MESH)
     length = ext.shape[1]
     edge = rows + HALO
     ext[:, edge:, :] = jnp.zeros((ext.shape[0], length - edge, 128), F32)
     pext[:, edge:, :] = jnp.zeros((2, length - edge, half), F32)
-    used = (atoms + 2 * RIM) * BMAX
-    padded[used:, :] = jnp.zeros((padded.shape[0] - used, padded.shape[1]), BF16)
-    ppadded[used:, :] = jnp.zeros((ppadded.shape[0] - used, ppadded.shape[1]), BF16)
-    low = (GROUP - 1) * GROUP
-    skew[:, 0:low, :] = jnp.zeros((skew.shape[0], low, 128), F32)
-    skew[:, low + K * GROUP:, :] = jnp.zeros((skew.shape[0], low, 128), F32)
+    low = (SUB - 1) * SUB
+    skew[:, :, 0:low, :] = jnp.zeros((*skew.shape[:2], low, 128), F32)
+    skew[:, :, low + K * SUB:, :] = jnp.zeros((*skew.shape[:2], low, 128), F32)
     pl.semaphore_wait(barrier, len(greeted))
 
     def remote(src, dst, sems, slot, target):
@@ -106,22 +103,18 @@
         remote(basis_hbm, counts.at[side], count_sems, (side,), (target, col))
         for side, target in ((0, up), (1, down))
     ]
-    for copy in count_copies:
-        copy.start()
-    pan_halos, vec_halos = [], []
+    pan_halos, passed, vec_halos = [], [], []
     for side, target in ((0, up), (1, down)):
         src_at = rows - HALO if side == 0 else 0
         dst_at = 0 if side == 0 else HALO + rows
-        for where in (0, 1):
-            to = col if where == 0 else other
-            pan_halos.append(remote(panel_hbm.at[pl.ds(src_at, HALO)], pan_ref.at[col, pl.ds(dst_at, HALO)],
-                                    pan_sems, (1 + 2 * side + where,), (target, to)))
+        pan_halos.append(remote(panel_hbm.at[pl.ds(src_at, HALO)], pan_ref.at[col, pl.ds(dst_at, HALO)],
+                                pan_sems, (1 + side,), (target, col)))
+        ghost = pan_ref.at[col, pl.ds(dst_at, HALO)]
+        passed.append(remote(ghost, ghost, pan_sems, (3 + side,), (row, other)))
         for piece in range(PIECES):
             part_at = piece * (HALO // PIECES)
             vec_halos.append(remote(vec_hbm.at[pl.ds(src_at + part_at, HALO // PIECES)],
                                     halo_ref.at[side, pl.ds(part_at, HALO // PIECES)], halo_sems, (side, piece), (target, col)))
-    for copy in pan_halos:
-        copy.start()
 
     own.wait()
     pan_t[pl.ds(pl.multiple_of(col * half, half), half), :] = pan_ref[col, body, :].T
@@ -133,18 +126,7 @@
     weight[...] = mask_ref[...].astype(F32) * occ_ref[...] / (vec_hbm.shape[1] * lax.axis_size("col"))
     for load in loads:
         load.wait()
-
-    lanes = [slice(c * 128, (c + 1) * 128) for c in range(ext.shape[0])]
-    chunk_rows = rows // 8
-
-    def widen(t, carry):
-        at = pl.multiple_of(t * chunk_rows, 16)
-        block = vec[pl.ds(at, chunk_rows), :].astype(F32)
-        for c, span in enumerate(lanes):
-            ext[c, pl.ds(HALO + at, chunk_rows), :] = block[:, span]
-        return carry
-
-    lax.fori_loop(0, 8, widen, 0)
+    blocks.start()
 
     swap.wait_recv()
     pan_t[pl.ds(pl.multiple_of(other * half, half), half), :] = pan_ref[other, body, :].T
@@ -213,92 +195,117 @@
         for step in first_steps(c):
             last_copy(c, step).wait_recv()
 
+    def greet_neighbours():
+        for copy in count_copies + pan_halos:
+            copy.start()
+
+    def pass_on():
+        for copy in pan_halos:
+            copy.wait_recv()
+        for copy in passed:
+            copy.start()
+
     def start_halos(*which):
         for piece in which:
             for copy in vec_halos[piece::PIECES]:
                 copy.start()
 
-    for first_c, last_c in ([(1, 3), (0, 1), (3, 4)] if chunks == 4 else [(0, chunks)]):
-        at = first_c * wide_c
-        inner = jnp.dot(pan_t[...], vec[:, at:last_c * wide_c], preferred_element_type=F32).T.astype(BF16)
-        for c in range(first_c, last_c):
-            part[c] = inner[c * wide_c - at:(c + 1) * wide_c - at]
+    for pair in ([(1, 2), (0, 3)] if chunks == 4 else [range(chunks)]):
+        columns = jnp.concatenate([vec[:, span_of(c)] for c in pair], axis=1)
+        inner = jnp.dot(pan_t[...], columns, preferred_element_type=F32).T.astype(BF16)
+        for at, c in enumerate(pair):
+            part[c] = inner[at * wide_c:(at + 1) * wide_c]
             for step in first_steps(c):
                 first_copy(c, step).start()
-    start_halos(0)
+
+    lanes = [slice(c * 128, (c + 1) * 128) for c in range(ext.shape[0])]
+    chunk_rows = rows // 8
+
+    def widen(t, carry):
+        at = pl.multiple_of(t * chunk_rows, 16)
+        block = vec[pl.ds(at, chunk_rows), :].astype(F32)
+        for c, span in enumerate(lanes):
+            ext[c, pl.ds(HALO + at, chunk_rows), :] = block[:, span]
+        return carry
+
+    lax.fori_loop(0, 8, widen, 0)
 
     for which in (0, 1):
         pext[which, HALO:HALO + rows, :] = pan_ref[which, body, :].astype(F32)
-    for copy in count_copies:
-        copy.wait_recv()
     here = basis_ref[...].astype(F32)
-    prev, post = counts[0].astype(F32), counts[1].astype(F32)
     lower = jnp.where(iota(atoms, atoms, 0) < iota(atoms, atoms, 1), 1.0, 0.0).astype(BF16)
-    table = jnp.concatenate([prev, here, post, jnp.zeros((5, atoms), F32)], axis=0).astype(BF16)
-    first = jnp.dot(table, lower, preferred_element_type=F32).astype(jnp.int32)
-    first_ref[...] = jnp.clip(first + (HALO - rows) + rows * iota(8, atoms, 0), 0, rows + 2 * HALO)
-    begin_copy = pltpu.make_async_copy(first_ref, starts, start_sem)
-    begin_copy.start()
-    lines = []
     at = iota(1, atoms, 1)
-    for k in range(K):
-        d = k - RIM
-        near = here
-        if d != 0:
-            turn = (-d) % atoms
-            inside = (at + d >= 0) & (at + d < atoms)
-            near = jnp.where(inside, pltpu.roll(here, turn, 1), pltpu.roll(prev if d < 0 else post, turn, 1))
-        lines.append(jnp.where(present_ref[k:k + 1, :] > 0, near, 0.0))
-    lines.append(proj_ref[...].astype(F32))
-    lines.append(jnp.zeros((atoms - K - 1, atoms), F32))
-    limit[...] = jnp.concatenate(lines, axis=0).T
+
+    def tables(prev, post, which):
+        table = jnp.concatenate([prev, here, post, jnp.zeros((5, atoms), F32)], axis=0).astype(BF16)
+        first = jnp.dot(table, lower, preferred_element_type=F32).astype(jnp.int32)
+        first_ref[which] = jnp.clip(first + (HALO - rows) + rows * iota(8, atoms, 0), 0, rows + 2 * HALO)
+        copy = pltpu.make_async_copy(first_ref.at[which], starts.at[which], start_sem.at[which])
+        copy.start()
+        lines = []
+        for k in range(K):
+            d = k - RIM
+            near = here
+            if d != 0:
+                turn = (-d) % atoms
+                inside = (at + d >= 0) & (at + d < atoms)
+                near = jnp.where(inside, pltpu.roll(here, turn, 1), pltpu.roll(prev if d < 0 else post, turn, 1))
+            lines.append(jnp.where(present_ref[k:k + 1, :] > 0, near, 0.0))
+        lines.append(proj_ref[...].astype(F32))
+        lines.append(jnp.zeros((atoms - K - 1, atoms), F32))
+        limit[...] = jnp.concatenate(lines, axis=0).T
+        return copy
+
+    none = jnp.zeros((1, atoms), F32)
+    begin_copy = tables(none, none, 0)
     blocks.wait()
 
-    in_i = group_of(GROUP, wide, 1, BMAX, NPMAX)
-    slot = (iota(GROUP, wide, 1) - BMAX * in_i).astype(F32)
+    in_i = group_of(SUB, wide, 1, BMAX, NPMAX)
+    slot = (iota(SUB, wide, 1) - BMAX * in_i).astype(F32)
     in_i = in_i.astype(F32)
     lane = iota(8, 128, 1)
+
+    def band_piece(u, i):
+        tiles = []
+        for tile in range(WIN // 128):
+            acc = None
+            for b in range(REACH):
+                to, last = max(b * BMAX, tile * 128), min((b + 1) * BMAX, (tile + 1) * 128)
+                while to < last:
+                    source = i * BMAX + to - b * BMAX
+                    count = min(last - to, 128 - source % 128)
+                    piece = skew[u, source // 128, pl.ds((REACH - 1 - b) * SUB, SUB, stride=SUB + 1), :]
+                    turn = (to - source) % 128
+                    piece = piece if turn == 0 else pltpu.roll(piece, turn, 1)
+                    acc = piece if acc is None else jnp.where(lane >= to % 128, piece, acc)
+                    to += count
+            tiles.append(acc)
+        return jnp.concatenate(tiles, axis=1)
 
     def band_step(t, carry):
         chunk = pl.ds(pl.multiple_of(t * GROUP, GROUP), GROUP)
         bounds = limit[chunk, :]
-        valid = in_i < bounds[:, K:K + 1]
-        for k in range(K):
-            block = cm_ref[k, chunk, :].astype(F32)
-            block = jnp.where(valid & (slot < bounds[:, k:k + 1]), block, 0.0)
-            top = (GROUP + K - 2 - k) * GROUP
-            for tile in range(wide // 128):
-                skew[tile, top:top + GROUP, :] = block[:, tile * 128:(tile + 1) * 128]
-        for i in range(NPMAX):
-            sides = []
-            for side in range(GROUP // 8):
-                near = range(8 * side, 8 * side + 8 + K - 1)
-                tiles = []
-                for tile in range(WIN // 128):
-                    acc, end = jnp.zeros((8, 128), F32), 0
-                    for b in near:
-                        to, last = max(b * BMAX, tile * 128), min((b + 1) * BMAX, (tile + 1) * 128)
-                        while to < last:
-                            source = i * BMAX + to - b * BMAX
-                            count = min(last - to, 128 - source % 128)
-                            begin = (REACH - 1 - b) * GROUP + 8 * side * (GROUP + 1)
-                            piece = skew[source // 128, pl.ds(begin, 8, stride=GROUP + 1), :]
-                            turn = (to - source) % 128
-                            piece = piece if turn == 0 else pltpu.roll(piece, turn, 1)
-                            acc = jnp.where(lane >= to % 128, piece, acc)
-                            to += count
-                            end = (to - 1) % 128 + 1
-                    tiles.append(jnp.where(lane < end, acc, 0.0) if 0 < end < 128 else acc)
-                sides.append(jnp.concatenate(tiles, axis=1))
-            band[t, i * GROUP:(i + 1) * GROUP, :] = jnp.concatenate(sides, axis=0).astype(BF16)
+        for u in range(GROUP // SUB):
+            within = bounds[u * SUB:(u + 1) * SUB]
+            valid = in_i < within[:, K:K + 1]
+            for k in range(K):
+                block = cm_ref[k, chunk, :].astype(F32)[u * SUB:(u + 1) * SUB]
+                block = jnp.where(valid & (slot < within[:, k:k + 1]), block, 0.0)
+                top = (REACH - 1 - k) * SUB
+                for tile in range(wide // 128):
+                    skew[u, tile, top:top + SUB, :] = block[:, tile * 128:(tile + 1) * 128]
+        for u in range(GROUP // SUB):
+            for i in range(0, NPMAX, 2):
+                both = jnp.concatenate([band_piece(u, i), band_piece(u, i + 1)], axis=0)
+                band[t * (GROUP // SUB) + u, i * SUB:(i + 2) * SUB, :] = both.astype(BF16)
         return carry
 
-    def gather(t, carry):
+    def gather(t, carry, which=0):
         at = pl.multiple_of(2 * t * BMAX, 16)
         begins = []
         for e in (0, 1):
             flat = 2 * t + e + atoms - RIM
-            begins.append(starts[lax.div(flat, atoms), lax.rem(flat, atoms)])
+            begins.append(starts[which, lax.div(flat, atoms), lax.rem(flat, atoms)])
         for c, span in enumerate(lanes):
             both = [ext[c, pl.ds(begin, BMAX), :] for begin in begins]
             padded[pl.ds(at, 2 * BMAX), span] = jnp.concatenate(both, axis=0).astype(BF16)
@@ -307,10 +314,10 @@
             ppadded[pl.ds(at, 2 * BMAX), c * half:(c + 1) * half] = jnp.concatenate(both, axis=0).astype(BF16)
         return carry
 
-    def project(g, carry):
-        at = pl.ds(pl.multiple_of(g * GROUP * BMAX, 16), WIN)
-        base[g] = jnp.dot(band[g], padded[at, :], preferred_element_type=F32)
-        lean[g] = jnp.dot(band[g], ppadded[at, :], preferred_element_type=F32).astype(BF16)
+    def project(s, carry=0):
+        at = pl.ds(pl.multiple_of(s * SUB * BMAX, 16), WIN)
+        base[s] = jnp.dot(band[s], padded[at, :], preferred_element_type=F32)
+        lean[s] = jnp.dot(band[s], ppadded[at, :], preferred_element_type=F32).astype(BF16)
         return carry
 
     def bands(low, high):
@@ -319,49 +326,65 @@
     def gathers(low, high):
         lax.fori_loop(low, high, gather, 0)
 
-    def projects(low, high):
-        lax.fori_loop(low, high, project, 0)
+    def projects(*which):
+        for s in which:
+            project(s)
 
     begin_copy.wait()
     inside_from, inside_to = RIM // 2, (atoms + RIM) // 2
     inside_mid = (inside_from + inside_to) // 2
-    eighth = groups // 4
-    works = [functools.partial(bands, t * eighth, (t + 1) * eighth) for t in range(4)]
+    def outer_bands():
+        for copy in count_copies:
+            copy.wait_recv()
+        tables(counts[0].astype(F32), counts[1].astype(F32), 1).wait()
+        lax.fori_loop(0, 2, lambda t, carry: band_step(t * (groups - 1), carry), 0)
+
+    third = (groups - 2) // 3
+    works = [functools.partial(bands, 1 + t * third, 1 + (t + 1) * third) for t in range(3)]
     works += [functools.partial(gathers, inside_from, inside_mid), functools.partial(gathers, inside_mid, inside_to)]
-    works += [functools.partial(projects, g, g + 1) for g in range(1, groups - 1)]
+    subs = atoms // SUB
+    works += [functools.partial(projects, s, s + 1) for s in range(2, subs - 2, 2)]
+    works += [outer_bands, functools.partial(projects, 1, subs - 2)]
     if chunks == 4:
         order = [
             [],
-            [(after_first, 1)],
+            [(after_first, 1), (greet_neighbours,), (start_halos, 0)],
             [(after_first, 0)],
-            [(after_fold, 1, 0)],
-            [(after_first, 2), (after_first, 3), (after_fold, 0, 0)],
+            [(after_fold, 1, 0), (after_first, 2), (start_halos, 1, 2)],
+            [(after_first, 3), (after_fold, 0, 0), (start_halos, 3)],
             [],
-            [(after_fold, 2, 0), (after_fold, 1, 1), (after_fold, 3, 0)],
+            [(after_fold, 2, 0)],
+            [(after_fold, 1, 1)],
+            [(after_fold, 3, 0)],
             [],
             [(after_fold, 0, 1), (after_fold, 2, 1)],
             [],
-            [(after_fold, 3, 1), (start_halos, 1, 2)],
-            [],
+            [(after_fold, 3, 1), (start_halos, 4, 5), (pass_on,)],
         ]
     else:
         every = range(chunks)
-        order = [[], [(after_first, c) for c in every] + [(start_halos, 1, 2)]]
+        order = [[], [(after_first, c) for c in every] + [(greet_neighbours,), (start_halos, *range(PIECES))]]
         order += [[(after_fold, c, turn) for c in every] for turn in range(len(rounds(0)))]
-        order += [[] for _ in works[len(order):]]
+        order += [[] for _ in works[len(order):-1]] + [[(pass_on,)]]
     for work, events in zip(works, order, strict=True):
         work()
         for event in events:
             event[0](*event[1:])
 
     size = GROUP * NPMAX
-    same = (iota(size, size, 0) & (GROUP - 1)) == (iota(size, size, 1) & (GROUP - 1))
-    expand = jnp.where(group_of(size, size, 0, GROUP, NPMAX) == (iota(size, size, 1) & (NPMAX - 1)), 1.0, 0.0).astype(BF16)
+    part_size = SUB * NPMAX
+    row_at, lane_at = iota(size, size, 0), iota(size, size, 1)
+    same = ((row_at >= part_size) == (lane_at >= part_size)) & ((row_at & (SUB - 1)) == (lane_at & (SUB - 1)))
+    expand = jnp.where(group_of(size, size, 0, SUB, size // SUB) - jnp.where(row_at >= part_size, NPMAX, 0)
+                       == (lane_at & (NPMAX - 1)), 1.0, 0.0).astype(BF16)
     owner = group_of(GROUP, size, 1, NPMAX, NPMAX)
+    pair_of = range(GROUP // SUB)
 
     def tail(span, g):
-        update = lax.dot_general(lean[g], mix_ref[span, :], across, preferred_element_type=F32)
-        rounded = (base[g, :, span] - update).astype(BF16)
+        lines = jnp.concatenate([lean[g * len(pair_of) + u] for u in pair_of], axis=0)
+        update = lax.dot_general(lines, mix_ref[span, :], across, preferred_element_type=F32)
+        plain = jnp.concatenate([base[g * len(pair_of) + u, :, span] for u in pair_of], axis=0)
+        rounded = (plain - update).astype(BF16)
         weighted = (rounded.astype(F32) * weight[:, span]).astype(BF16)
         return lax.dot_general(weighted, rounded, across, preferred_element_type=F32)
 
@@ -372,7 +395,8 @@
         spread = jnp.dot(top, expand, preferred_element_type=F32) + jnp.dot(rest, expand, preferred_element_type=F32)
         result = jnp.zeros((GROUP, size), F32)
         for i in range(NPMAX):
-            result = jnp.where(owner == i, spread[i * GROUP:(i + 1) * GROUP, :], result)
+            rows_of = [spread[u * part_size + i * SUB:u * part_size + (i + 1) * SUB, :] for u in pair_of]
+            result = jnp.where(owner == i, jnp.concatenate(rows_of, axis=0), result)
         dens[pl.ds(pl.multiple_of(g * GROUP, GROUP), GROUP), :] = result
 
     cut = vec.shape[1] // 2
@@ -408,7 +432,9 @@
     sent = [den_copy(other * share + GROUP * col, inside, 0), den_copy(other * (atoms - GROUP), GROUP, 1)]
     sent[0].start()
 
-    for copy in pan_halos + vec_halos:
+    for copy in pan_halos:
+        copy.wait_send()
+    for copy in passed + vec_halos:
         copy.wait()
     for side, at in ((0, 0), (1, HALO + rows)):
         block = halo_ref[side].astype(F32)
@@ -416,14 +442,15 @@
             ext[c, at:at + HALO, :] = block[:, span]
         for which in (0, 1):
             pext[which, at:at + HALO, :] = pan_ref[which, at:at + HALO, :].astype(F32)
-    lax.fori_loop(0, RIM // 2, gather, 0)
-    lax.fori_loop((atoms + RIM) // 2, (atoms + 2 * RIM) // 2, gather, 0)
+    late_gather = functools.partial(gather, which=1)
+    lax.fori_loop(0, RIM // 2, late_gather, 0)
+    lax.fori_loop((atoms + RIM) // 2, (atoms + 2 * RIM) // 2, late_gather, 0)
 
     every = slice(0, 2 * cut)
+    project(other * (subs - 1))
     theirs, ours = other * (groups - 1), col * (groups - 1)
-    project(theirs, 0)
     product = tail(every, theirs)
-    project(ours, 0)
+    project(col * (subs - 1))
     finish(product, theirs)
     sent[1].start()
     finish(tail(every, ours), ours)
@@ -477,7 +504,8 @@
     unit = width // n
     turns = most.bit_length() - 1
     ext_rows = rows + 2 * HALO
-    pad_rows = (groups - 1) * GROUP * BMAX + WIN
+    subs = atoms // SUB
+    pad_rows = (subs - 1) * SUB * BMAX + WIN
     dma = pltpu.SemaphoreType.DMA
     operands = (vectors_in, panel, jnp.swapaxes(coupling, 0, 1), factor, atom_basis, proj_count[None, :], block_present.T,
                 occ_mask[None, :], occ_weight[None, :])
@@ -506,20 +534,20 @@
             pltpu.VMEM((atoms, atoms), F32),
             pltpu.VMEM((K, atoms, wide), BF16),
             pltpu.VMEM((2, HALO, cols), BF16),
-            pltpu.VMEM((wide // 128, (2 * GROUP + K - 2) * GROUP, 128), F32),
-            pltpu.VMEM((groups, GROUP * NPMAX, WIN), BF16),
-            pltpu.VMEM((8, atoms), jnp.int32),
-            pltpu.SMEM((8, atoms), jnp.int32),
+            pltpu.VMEM((GROUP // SUB, wide // 128, (2 * SUB + K - 2) * SUB, 128), F32),
+            pltpu.VMEM((subs, SUB * NPMAX, WIN), BF16),
+            pltpu.VMEM((2, 8, atoms), jnp.int32),
+            pltpu.SMEM((2, 8, atoms), jnp.int32),
             pltpu.VMEM((cols // 128, ext_rows + BMAX, 128), F32),
             pltpu.VMEM((2, ext_rows + BMAX, half), F32),
             pltpu.VMEM((pad_rows, cols), BF16),
             pltpu.VMEM((pad_rows, npan), BF16),
-            pltpu.VMEM((groups, GROUP * NPMAX, cols), F32),
-            pltpu.VMEM((groups, GROUP * NPMAX, npan), BF16),
+            pltpu.VMEM((subs, SUB * NPMAX, cols), F32),
+            pltpu.VMEM((subs, SUB * NPMAX, npan), BF16),
             pltpu.VMEM((groups, GROUP * NPMAX, GROUP * NPMAX), F32),
             pltpu.VMEM((atoms, NPMAX * NPMAX), F32),
             pltpu.VMEM((1, cols), F32),
-            dma((2,)), dma((6,)), dma, dma, dma, dma((2, 5)), dma((2, 2, PIECES)), dma((2, 2)),
+            dma((2,)), dma((6,)), dma, dma, dma((2,)), dma((2, 5)), dma((2, 2, PIECES)), dma((2, 2)),
             dma((2, chunks, 2, most)), dma((2, chunks, turns)), dma((2, 2)),
         ],
         compiler_params=pltpu.CompilerParams(collective_id=0, has_side_effects=True, vmem_limit_bytes=48 << 20),

time: 40.5 us -> 38.8 us (0.958)
  Pallas kernels: 39.7 us -> 38 us
    pallas_call x1, Pallas kernels: 36.7 us -> 35 us  [local(): pl.pallas_call(functools.partial(mix_kernel, n, plane), out_shape=(jax.Sh...]
where the time goes in v3:
time: 38.8 us; the launch traced here: 38.7 us
  Pallas kernels  38 us (98%)
  between operations  0.64 us (2%)
    pallas_call x1, Pallas kernels, local(): pl.pallas_call(functools.partial(mix_kernel, n, plane), out_shape=(jax.Sh...  35 us
    pallas_call x1, Pallas kernels, local(): pl.pallas_call(vector_kernel, out_shape=(jax.ShapeDtypeStruct((rows, cols...  3.04 us

profile of v3, /device:TPU:0, one launch (start us, length us, event | category | flops | bytes accessed | tf_op | source)
XLA Modules:
  0.0 38.7 jit_solution(4772888051995487253)
XLA Ops:
  0.6 35.0 %shard_map.104 = (bf16[2048,1024]{1,0:T(8,128)(2,1)S(1)}, bf16[2,2240,128]{2,1,0:T(8,128)(2,1)S(1)}, bf16[1024,256]{1,0:T(8,128)(2,1)S(1)}, f32[64,256]{1,0:T(8,128)S(1)}, f32[64,256]{1,0:T(8,128)S(1)}) custom-call(bf16[2048,1024]{1,0:T(8,128)(2,1)} %vec_hbm.1, bf16[2048,128]{1,0:T(8,128)(2,1)} %panel_hbm.1, bf16[9,128,384]{2,1,0:T(8,128)(2,1)} %bitcast.5, ...), custom_call_target="tpu_custom_call" | custom-call | flops 8000000000 | bytes 10485760 | tf_op jit(solution)/shard_map/pallas_call | solution.py:513
  35.6 3.0 %shard_map.105 = (bf16[2048,1024]{1,0:T(8,128)(2,1)}, f32[64,256]{1,0:T(8,128)}) custom-call(bf16[2048,1024]{1,0:T(8,128)(2,1)S(1)} %get-tuple-element.7.vin_ref, bf16[2,2240,128]{2,1,0:T(8,128)(2,1)S(1)} %get-tuple-element.8.pan_ref, bf16[1024,256]{1,0:T(8,128)(2,1)S(1)} %get-tuple-element.9.mix_ref, f32[64,256]{1,0:T(8,128)S(1)} %get-tuple-element.10.own_ref, ...), custom_call_target="tpu_custom_call" | custom-call | flops 6000000000 | bytes 10485760 | tf_op jit(solution)/shard_map/pallas_call | solution.py:557

commit v4 on v3

--- a/solution.py
+++ b/solution.py
@@ -13,6 +13,7 @@
 RIM = (K - 1) // 2
 HALO = RIM * BMAX
 PIECES = 6
+HALO_ORDER = (0, 6, 1, 7, 2, 8, 3, 9, 4, 5, 10, 11)
 GROUP = 16
 SUB = 8
 WIN = -(-(SUB + K - 1) * BMAX // 128) * 128
@@ -111,10 +112,15 @@
                                 pan_sems, (1 + side,), (target, col)))
         ghost = pan_ref.at[col, pl.ds(dst_at, HALO)]
         passed.append(remote(ghost, ghost, pan_sems, (3 + side,), (row, other)))
+    far = jnp.where(row == n - 1, 0, 1)
+    for side in (far, 1 - far):
+        target = jnp.where(side == 0, up, down)
+        src_at = (rows - HALO) * (1 - side)
         for piece in range(PIECES):
             part_at = piece * (HALO // PIECES)
-            vec_halos.append(remote(vec_hbm.at[pl.ds(src_at + part_at, HALO // PIECES)],
-                                    halo_ref.at[side, pl.ds(part_at, HALO // PIECES)], halo_sems, (side, piece), (target, col)))
+            src = pl.ds(pl.multiple_of(src_at + part_at, HALO // PIECES), HALO // PIECES)
+            vec_halos.append(remote(vec_hbm.at[src], halo_ref.at[side, pl.ds(part_at, HALO // PIECES)],
+                                    halo_sems, (side, piece), (target, col)))
 
     own.wait()
     pan_t[pl.ds(pl.multiple_of(col * half, half), half), :] = pan_ref[col, body, :].T
@@ -207,7 +213,7 @@
 
     def start_halos(*which):
         for piece in which:
-            for copy in vec_halos[piece::PIECES]:
+            for copy in [vec_halos[i] for i in HALO_ORDER[2 * piece:2 * piece + 2]]:
                 copy.start()
 
     for pair in ([(1, 2), (0, 3)] if chunks == 4 else [range(chunks)]):
@@ -333,10 +339,12 @@
     begin_copy.wait()
     inside_from, inside_to = RIM // 2, (atoms + RIM) // 2
     inside_mid = (inside_from + inside_to) // 2
+    late_copy = []
+
     def outer_bands():
         for copy in count_copies:
             copy.wait_recv()
-        tables(counts[0].astype(F32), counts[1].astype(F32), 1).wait()
+        late_copy.append(tables(counts[0].astype(F32), counts[1].astype(F32), 1))
         lax.fori_loop(0, 2, lambda t, carry: band_step(t * (groups - 1), carry), 0)
 
     third = (groups - 2) // 3
@@ -350,16 +358,16 @@
             [],
             [(after_first, 1), (greet_neighbours,), (start_halos, 0)],
             [(after_first, 0)],
-            [(after_fold, 1, 0), (after_first, 2), (start_halos, 1, 2)],
-            [(after_first, 3), (after_fold, 0, 0), (start_halos, 3)],
+            [(after_fold, 1, 0), (after_first, 2), (after_first, 3), (start_halos, 1, 2)],
+            [(after_fold, 0, 0), (start_halos, 3)],
             [],
             [(after_fold, 2, 0)],
-            [(after_fold, 1, 1)],
-            [(after_fold, 3, 0)],
+            [(after_fold, 1, 1), (after_fold, 3, 0)],
             [],
-            [(after_fold, 0, 1), (after_fold, 2, 1)],
+            [(after_fold, 0, 1)],
+            [(after_fold, 2, 1), (after_fold, 3, 1), (start_halos, 4, 5), (pass_on,)],
             [],
-            [(after_fold, 3, 1), (start_halos, 4, 5), (pass_on,)],
+            [],
         ]
     else:
         every = range(chunks)
@@ -401,7 +409,7 @@
 
     cut = vec.shape[1] // 2
     first_half, second_half = slice(0, cut), slice(cut, 2 * cut)
-    batch = max(d for d in (3, 2, 1) if (groups - 2) % d == 0)
+    batch = max(d for d in (6, 3, 2, 1) if (groups - 2) % d == 0)
 
     def tail_first(t, carry):
         for e in range(batch):
@@ -442,6 +450,7 @@
             ext[c, at:at + HALO, :] = block[:, span]
         for which in (0, 1):
             pext[which, at:at + HALO, :] = pan_ref[which, at:at + HALO, :].astype(F32)
+    late_copy[0].wait()
     late_gather = functools.partial(gather, which=1)
     lax.fori_loop(0, RIM // 2, late_gather, 0)
     lax.fori_loop((atoms + RIM) // 2, (atoms + 2 * RIM) // 2, late_gather, 0)

time: 38.8 us -> 38 us (0.979)
  Pallas kernels: 38 us -> 37.2 us
    pallas_call x1, Pallas kernels: 35 us -> 34.2 us  [local(): pl.pallas_call(functools.partial(mix_kernel, n, plane), out_shape=(jax.Sh...]
where the time goes in v4:
time: 38 us; the launch traced here: 37.8 us
  Pallas kernels  37.2 us (98%)
  between operations  0.64 us (2%)
    pallas_call x1, Pallas kernels, local(): pl.pallas_call(functools.partial(mix_kernel, n, plane), out_shape=(jax.Sh...  34.2 us
    pallas_call x1, Pallas kernels, local(): pl.pallas_call(vector_kernel, out_shape=(jax.ShapeDtypeStruct((rows, cols...  3.04 us

profile of v4, /device:TPU:0, one launch (start us, length us, event | category | flops | bytes accessed | tf_op | source)
XLA Modules:
  0.0 37.8 jit_solution(5532645498267305223)
XLA Ops:
  0.6 34.2 %shard_map.104 = (bf16[2048,1024]{1,0:T(8,128)(2,1)S(1)}, bf16[2,2240,128]{2,1,0:T(8,128)(2,1)S(1)}, bf16[1024,256]{1,0:T(8,128)(2,1)S(1)}, f32[64,256]{1,0:T(8,128)S(1)}, f32[64,256]{1,0:T(8,128)S(1)}) custom-call(bf16[2048,1024]{1,0:T(8,128)(2,1)} %vec_hbm.1, bf16[2048,128]{1,0:T(8,128)(2,1)} %panel_hbm.1, bf16[9,128,384]{2,1,0:T(8,128)(2,1)} %bitcast.5, ...), custom_call_target="tpu_custom_call" | custom-call | flops 8000000000 | bytes 10485760 | tf_op jit(solution)/shard_map/pallas_call | solution.py:522
  34.8 3.0 %shard_map.105 = (bf16[2048,1024]{1,0:T(8,128)(2,1)}, f32[64,256]{1,0:T(8,128)}) custom-call(bf16[2048,1024]{1,0:T(8,128)(2,1)S(1)} %get-tuple-element.7.vin_ref, bf16[2,2240,128]{2,1,0:T(8,128)(2,1)S(1)} %get-tuple-element.8.pan_ref, bf16[1024,256]{1,0:T(8,128)(2,1)S(1)} %get-tuple-element.9.mix_ref, f32[64,256]{1,0:T(8,128)S(1)} %get-tuple-element.10.own_ref, ...), custom_call_target="tpu_custom_call" | custom-call | flops 6000000000 | bytes 10485760 | tf_op jit(solution)/shard_map/pallas_call | solution.py:566

commit v5 on v4

--- a/solution.py
+++ b/solution.py
@@ -134,11 +134,22 @@
         load.wait()
     blocks.start()
 
+    def span_of(c):
+        return slice(c * wide_c, (c + 1) * wide_c)
+
+    pairs = [(1, 2), (0, 3)] if chunks == 4 else [range(chunks)]
+
+    def products(pair, which):
+        mine = pl.ds(pl.multiple_of(which * half, half), half)
+        columns = jnp.concatenate([vec[:, span_of(c)] for c in pair], axis=1)
+        inner = jnp.dot(pan_t[mine, :], columns, preferred_element_type=F32).T.astype(BF16)
+        for at, c in enumerate(pair):
+            part[c, :, mine] = inner[at * wide_c:(at + 1) * wide_c]
+
+    for pair in pairs:
+        products(pair, col)
     swap.wait_recv()
     pan_t[pl.ds(pl.multiple_of(other * half, half), half), :] = pan_ref[other, body, :].T
-
-    def span_of(c):
-        return slice(c * wide_c, (c + 1) * wide_c)
 
     def first_copy(c, step):
         (size, at, peer), (size_s, _, _) = ways[c]
@@ -216,11 +227,9 @@
             for copy in [vec_halos[i] for i in HALO_ORDER[2 * piece:2 * piece + 2]]:
                 copy.start()
 
-    for pair in ([(1, 2), (0, 3)] if chunks == 4 else [range(chunks)]):
-        columns = jnp.concatenate([vec[:, span_of(c)] for c in pair], axis=1)
-        inner = jnp.dot(pan_t[...], columns, preferred_element_type=F32).T.astype(BF16)
-        for at, c in enumerate(pair):
-            part[c] = inner[at * wide_c:(at + 1) * wide_c]
+    for pair in pairs:
+        products(pair, other)
+        for c in pair:
             for step in first_steps(c):
                 first_copy(c, step).start()
 
@@ -359,9 +368,9 @@
             [(after_first, 1), (greet_neighbours,), (start_halos, 0)],
             [(after_first, 0)],
             [(after_fold, 1, 0), (after_first, 2), (after_first, 3), (start_halos, 1, 2)],
-            [(after_fold, 0, 0), (start_halos, 3)],
+            [(after_fold, 0, 0)],
             [],
-            [(after_fold, 2, 0)],
+            [(after_fold, 2, 0), (start_halos, 3)],
             [(after_fold, 1, 1), (after_fold, 3, 0)],
             [],
             [(after_fold, 0, 1)],
@@ -411,10 +420,11 @@
     first_half, second_half = slice(0, cut), slice(cut, 2 * cut)
     batch = max(d for d in (6, 3, 2, 1) if (groups - 2) % d == 0)
 
-    def tail_first(t, carry):
+    def tail_first(span, t, carry, fresh=True):
         for e in range(batch):
             g = 1 + t * batch + e
-            full[g] = tail(first_half, g)
+            product = tail(span, g)
+            full[g] = product if fresh else full[g] + product
         return carry
 
     def tail_second(t, carry):
@@ -423,9 +433,10 @@
             finish(product, 1 + t * batch + e)
         return carry
 
-    for c in range(0, max(1, chunks // 2)):
+    for c in (1, 0) if chunks == 4 else (0,):
         after_last(c)
-    lax.fori_loop(0, (groups - 2) // batch, tail_first, 0)
+        span = span_of(c) if chunks == 4 else first_half
+        lax.fori_loop(0, (groups - 2) // batch, functools.partial(tail_first, span, fresh=c == 1 or chunks != 4), 0)
     for c in range(max(1, chunks // 2), chunks):
         after_last(c)
     lax.fori_loop(0, (groups - 2) // batch, tail_second, 0)

time: 38 us -> 37.5 us (0.987)
  Pallas kernels: 37.2 us -> 36.7 us
    pallas_call x1, Pallas kernels: 34.2 us -> 33.7 us  [local(): pl.pallas_call(functools.partial(mix_kernel, n, plane), out_shape=(jax.Sh...]
where the time goes in v5:
time: 37.5 us; the launch traced here: 37.4 us
  Pallas kernels  36.7 us (98%)
  between operations  0.64 us (2%)
    pallas_call x1, Pallas kernels, local(): pl.pallas_call(functools.partial(mix_kernel, n, plane), out_shape=(jax.Sh...  33.7 us
    pallas_call x1, Pallas kernels, local(): pl.pallas_call(vector_kernel, out_shape=(jax.ShapeDtypeStruct((rows, cols...  3.04 us

profile of v5, /device:TPU:0, one launch (start us, length us, event | category | flops | bytes accessed | tf_op | source)
XLA Modules:
  0.0 37.4 jit_solution(16176473185881735817)
XLA Ops:
  0.6 33.7 %shard_map.104 = (bf16[2048,1024]{1,0:T(8,128)(2,1)S(1)}, bf16[2,2240,128]{2,1,0:T(8,128)(2,1)S(1)}, bf16[1024,256]{1,0:T(8,128)(2,1)S(1)}, f32[64,256]{1,0:T(8,128)S(1)}, f32[64,256]{1,0:T(8,128)S(1)}) custom-call(bf16[2048,1024]{1,0:T(8,128)(2,1)} %vec_hbm.1, bf16[2048,128]{1,0:T(8,128)(2,1)} %panel_hbm.1, bf16[9,128,384]{2,1,0:T(8,128)(2,1)} %bitcast.5, ...), custom_call_target="tpu_custom_call" | custom-call | flops 8000000000 | bytes 10485760 | tf_op jit(solution)/shard_map/pallas_call | solution.py:533
  34.3 3.0 %shard_map.105 = (bf16[2048,1024]{1,0:T(8,128)(2,1)}, f32[64,256]{1,0:T(8,128)}) custom-call(bf16[2048,1024]{1,0:T(8,128)(2,1)S(1)} %get-tuple-element.7.vin_ref, bf16[2,2240,128]{2,1,0:T(8,128)(2,1)S(1)} %get-tuple-element.8.pan_ref, bf16[1024,256]{1,0:T(8,128)(2,1)S(1)} %get-tuple-element.9.mix_ref, f32[64,256]{1,0:T(8,128)S(1)} %get-tuple-element.10.own_ref, ...), custom_call_target="tpu_custom_call" | custom-call | flops 6000000000 | bytes 10485760 | tf_op jit(solution)/shard_map/pallas_call | solution.py:577

commit v6 on v5

--- a/solution.py
+++ b/solution.py
@@ -222,6 +222,12 @@
         for copy in passed:
             copy.start()
 
+    def slow_halos(*which):
+        pl.when(col == 0)(lambda: start_halos(*which))
+
+    def fast_halos(*which):
+        pl.when(col == 1)(lambda: start_halos(*which))
+
     def start_halos(*which):
         for piece in which:
             for copy in [vec_halos[i] for i in HALO_ORDER[2 * piece:2 * piece + 2]]:
@@ -374,8 +380,8 @@
             [(after_fold, 1, 1), (after_fold, 3, 0)],
             [],
             [(after_fold, 0, 1)],
-            [(after_fold, 2, 1), (after_fold, 3, 1), (start_halos, 4, 5), (pass_on,)],
-            [],
+            [(after_fold, 2, 1), (after_fold, 3, 1), (slow_halos, 4, 5), (pass_on,)],
+            [(fast_halos, 4, 5)],
             [],
         ]
     else:

time: 37.5 us -> 37.1 us (0.989)
    pallas_call x1, Pallas kernels: 33.7 us -> 33.3 us  [local(): pl.pallas_call(functools.partial(mix_kernel, n, plane), out_shape=(jax.Sh...]
where the time goes in v6:
time: 37.1 us; the launch traced here: 37 us
  Pallas kernels  36.4 us (98%)
  between operations  0.64 us (2%)
    pallas_call x1, Pallas kernels, local(): pl.pallas_call(functools.partial(mix_kernel, n, plane), out_shape=(jax.Sh...  33.3 us
    pallas_call x1, Pallas kernels, local(): pl.pallas_call(vector_kernel, out_shape=(jax.ShapeDtypeStruct((rows, cols...  3.04 us

profile of v6, /device:TPU:0, one launch (start us, length us, event | category | flops | bytes accessed | tf_op | source)
XLA Modules:
  0.0 37.0 jit_solution(5409053859276005937)
XLA Ops:
  0.6 33.3 %shard_map.104 = (bf16[2048,1024]{1,0:T(8,128)(2,1)S(1)}, bf16[2,2240,128]{2,1,0:T(8,128)(2,1)S(1)}, bf16[1024,256]{1,0:T(8,128)(2,1)S(1)}, f32[64,256]{1,0:T(8,128)S(1)}, f32[64,256]{1,0:T(8,128)S(1)}) custom-call(bf16[2048,1024]{1,0:T(8,128)(2,1)} %vec_hbm.1, bf16[2048,128]{1,0:T(8,128)(2,1)} %panel_hbm.1, bf16[9,128,384]{2,1,0:T(8,128)(2,1)} %bitcast.5, ...), custom_call_target="tpu_custom_call" | custom-call | flops 8000000000 | bytes 10485760 | tf_op jit(solution)/shard_map/pallas_call | solution.py:539
  34.0 3.0 %shard_map.105 = (bf16[2048,1024]{1,0:T(8,128)(2,1)}, f32[64,256]{1,0:T(8,128)}) custom-call(bf16[2048,1024]{1,0:T(8,128)(2,1)S(1)} %get-tuple-element.7.vin_ref, bf16[2,2240,128]{2,1,0:T(8,128)(2,1)S(1)} %get-tuple-element.8.pan_ref, bf16[1024,256]{1,0:T(8,128)(2,1)S(1)} %get-tuple-element.9.mix_ref, f32[64,256]{1,0:T(8,128)S(1)} %get-tuple-element.10.own_ref, ...), custom_call_target="tpu_custom_call" | custom-call | flops 6000000000 | bytes 10485760 | tf_op jit(solution)/shard_map/pallas_call | solution.py:583

commit v7 on v6

--- a/solution.py
+++ b/solution.py
@@ -381,8 +381,8 @@
             [],
             [(after_fold, 0, 1)],
             [(after_fold, 2, 1), (after_fold, 3, 1), (slow_halos, 4, 5), (pass_on,)],
+            [],
             [(fast_halos, 4, 5)],
-            [],
         ]
     else:
         every = range(chunks)

time: 37.1 us -> 37 us (level)
  no operation moved by 1% of the time
where the time goes in v7:
time: 37 us; the launch traced here: 36.8 us
  Pallas kernels  36.2 us (98%)
  between operations  0.64 us (2%)
    pallas_call x1, Pallas kernels, local(): pl.pallas_call(functools.partial(mix_kernel, n, plane), out_shape=(jax.Sh...  33.1 us
    pallas_call x1, Pallas kernels, local(): pl.pallas_call(vector_kernel, out_shape=(jax.ShapeDtypeStruct((rows, cols...  3.04 us

profile of v7, /device:TPU:0, one launch (start us, length us, event | category | flops | bytes accessed | tf_op | source)
XLA Modules:
  0.0 36.8 jit_solution(16265337763792024622)
XLA Ops:
  0.6 33.1 %shard_map.104 = (bf16[2048,1024]{1,0:T(8,128)(2,1)S(1)}, bf16[2,2240,128]{2,1,0:T(8,128)(2,1)S(1)}, bf16[1024,256]{1,0:T(8,128)(2,1)S(1)}, f32[64,256]{1,0:T(8,128)S(1)}, f32[64,256]{1,0:T(8,128)S(1)}) custom-call(bf16[2048,1024]{1,0:T(8,128)(2,1)} %vec_hbm.1, bf16[2048,128]{1,0:T(8,128)(2,1)} %panel_hbm.1, bf16[9,128,384]{2,1,0:T(8,128)(2,1)} %bitcast.5, ...), custom_call_target="tpu_custom_call" | custom-call | flops 8000000000 | bytes 10485760 | tf_op jit(solution)/shard_map/pallas_call | solution.py:539
  33.8 3.0 %shard_map.105 = (bf16[2048,1024]{1,0:T(8,128)(2,1)}, f32[64,256]{1,0:T(8,128)}) custom-call(bf16[2048,1024]{1,0:T(8,128)(2,1)S(1)} %get-tuple-element.7.vin_ref, bf16[2,2240,128]{2,1,0:T(8,128)(2,1)S(1)} %get-tuple-element.8.pan_ref, bf16[1024,256]{1,0:T(8,128)(2,1)S(1)} %get-tuple-element.9.mix_ref, f32[64,256]{1,0:T(8,128)S(1)} %get-tuple-element.10.own_ref, ...), custom_call_target="tpu_custom_call" | custom-call | flops 6000000000 | bytes 10485760 | tf_op jit(solution)/shard_map/pallas_call | solution.py:583
